TPU v7x, 128 devices: a whole 4x4x4 slice. The times are simulated.
128 devices in a mesh: dp: 8 (over z, x_hi), mp: 16 (over y, x_lo, core).
Axes of the slice: x: 4 (x_hi: 2, x_lo: 2; x = x_hi * 2 + x_lo), y: 4, z: 4, core: 2. Of those that a mesh axis runs over, the one named last changes fastest.
Arguments:
- tokens: bfloat16 [16384, 2048], P(('dp', 'mp')), may hold values from -6 to 6
- attn_gain: float32 [2048], replicated, may hold values from 0.25 to 1.75
- mlp_gain: float32 [2048], replicated, may hold values from 0.25 to 1.75
- query_weight: bfloat16 [2048, 2048], replicated, as said below
- keyval_weight: bfloat16 [2048, 1024], replicated, as said below
- output_weight: bfloat16 [2048, 2048], replicated, may hold values from -0.125 to 0.125
- gate_rows: float32 [2048, 8192], P(('dp', 'mp')), may hold values from -0.125 to 0.125
- up_rows: float32 [2048, 8192], P(('dp', 'mp')), may hold values from -0.125 to 0.125
- down_rows: float32 [8192, 2048], P(('dp', 'mp')), may hold values from -0.0625 to 0.0625
- lengths: int32 [8, 1], P('dp'), may hold values from 1024 to 2048
- valid: int32 [16384], P(('dp', 'mp')), may hold values 0 or 1
- page_table: int32 [1024, 1], P(('dp', 'mp')), may hold values from 0 to 7; in each aligned block of 8 rows (0 to 7, 8 to 15, ...) at most 2 rows name the same one
Outputs:
- layer_out: bfloat16 [16384, 2048], P(('dp', 'mp'))
- page_cache: bfloat16 [8, 16, 8, 2, 16, 1024], P('dp', 'mp')
Inputs may be any that keep to these rules, and one draw needn't show every extreme that they name: `page_table`: of the 8 pages of one device at most 2 name the same holder; in every draw some device sends 2 pages to one holder. `query_weight`: entries are independent, of mean zero. `keyval_weight`: entries are independent, of mean zero.
All inputs are finite; a program needn't handle non-finite values. No bound on the sum of `valid` on one device may be relied on, other than what follows from the above.
Results may differ from a plain program's by a relative error of at most 0.02.
The roundings to bfloat16 on the way count: a program that leaves them out, or rounds other values in their place, can miss the bound.
Values may be sent and summed in bfloat16 or wider, within the bound.
A program may use at most 128 MiB of HBM per device.

v0:
```python
import jax
import jax.numpy as jnp
from jax import lax
from jax.sharding import PartitionSpec as P

QH = 32
KVH = 8
HD = 64
PAGE = 16
PAGE_MOST = 2


rope_base = 500000.0


def rms_scale(values, gain):
    mean_square = jnp.mean(values * values, axis=-1, keepdims=True)
    return values * lax.rsqrt(mean_square + 1e-05) * gain


def prompt_ids(lens, rows):
    ends = jnp.cumsum(lens)
    starts = ends - lens
    segment = jnp.sum((rows[:, None] >= ends[None, :]).astype(jnp.int32), axis=1)
    prompt_range = jnp.arange(lens.shape[0], dtype=jnp.int32)
    first = jnp.sum(
        jnp.where(segment[:, None] == prompt_range[None, :], starts[None, :], 0), axis=1
    )
    return (segment, rows - first)


def rotate(heads, position):
    half = heads.shape[-1] // 2
    expo = jnp.arange(half, dtype=jnp.float32) * (2.0 / heads.shape[-1])
    inverse = jnp.exp(-expo * jnp.log(jnp.float32(rope_base)))
    angle = position.astype(jnp.float32)[:, None] * inverse[None, :]
    cosine = jnp.cos(angle)[:, None, :]
    sine = jnp.sin(angle)[:, None, :]
    first_half = heads[..., :half]
    second_half = heads[..., half:]
    return jnp.concatenate(
        [first_half * cosine - second_half * sine, second_half * cosine + first_half * sine],
        axis=-1,
    )


def on_device(
    tokens,
    attn_gain,
    mlp_gain,
    query_weight,
    keyval_weight,
    output_weight,
    gate_rows,
    up_rows,
    down_rows,
    lengths,
    valid,
    page_table,
):
    mp_count = lax.axis_size("mp")
    dp_count = lax.axis_size("dp")
    column = lax.axis_index("mp")
    tok_dev = tokens.shape[0]
    tok_grp = tok_dev * mp_count
    heads_dev = QH // mp_count
    lens = lengths[0]
    local_rows = column * tok_dev + jnp.arange(tok_dev, dtype=jnp.int32)
    unused_segment, position = prompt_ids(lens, local_rows)
    tokens_f = tokens.astype(jnp.float32)
    normed = rms_scale(tokens_f, attn_gain).astype(jnp.bfloat16)
    queries = jnp.dot(normed, query_weight, preferred_element_type=jnp.float32).reshape(
        tok_dev, QH, HD
    )
    queries = rotate(queries, position).astype(jnp.bfloat16)
    keyval = jnp.dot(normed, keyval_weight, preferred_element_type=jnp.float32)
    keys = rotate(keyval[:, : KVH * HD].reshape(tok_dev, KVH, HD), position).astype(jnp.bfloat16)
    values = keyval[:, KVH * HD :].reshape(tok_dev, KVH, HD).astype(jnp.bfloat16)
    query_send = queries.reshape(tok_dev, mp_count, heads_dev * HD)
    pair_send = jnp.repeat(jnp.concatenate([keys, values], axis=-1), mp_count // KVH, axis=1)
    flag_send = jnp.broadcast_to(valid.astype(jnp.bfloat16)[:, None, None], (tok_dev, mp_count, 1))
    query_in, pair_in, flag_in = (
        lax.all_to_all(query_send, "mp", split_axis=1, concat_axis=0, tiled=True),
        lax.all_to_all(pair_send, "mp", split_axis=1, concat_axis=0, tiled=True),
        lax.all_to_all(flag_send, "mp", split_axis=1, concat_axis=0, tiled=True),
    )
    query_in = query_in.reshape(tok_grp, heads_dev, HD)
    key_in = pair_in[:, 0, :HD]
    value_in = pair_in[:, 0, HD:]
    key_open = flag_in[:, 0, 0] > 0.5
    group_rows = jnp.arange(tok_grp, dtype=jnp.int32)
    segment_all, unused_position = prompt_ids(lens, group_rows)
    block_rows = min(512, tok_grp)

    def attend_block(block_index):
        start = block_index * block_rows
        query_block = lax.dynamic_slice_in_dim(query_in, start, block_rows, 0)
        query_rows = start + jnp.arange(block_rows, dtype=jnp.int32)
        query_segment = lax.dynamic_slice_in_dim(segment_all, start, block_rows, 0)
        scores = (
            jnp.einsum("thd,sd->hts", query_block, key_in, preferred_element_type=jnp.float32)
            * 0.125
        )
        allowed = (
            (query_segment[:, None] == segment_all[None, :])
            & (group_rows[None, :] <= query_rows[:, None])
            & (key_open[None, :] | (group_rows[None, :] == query_rows[:, None]))
        )
        scores = jnp.where(allowed[None], scores, jnp.float32(-1e30))
        top = jnp.max(scores, axis=-1, keepdims=True)
        expd = jnp.exp(scores - top)
        weights = (expd / jnp.sum(expd, axis=-1, keepdims=True)).astype(jnp.bfloat16)
        mixed = jnp.einsum("hts,sd->thd", weights, value_in, preferred_element_type=jnp.float32)
        return mixed.astype(jnp.bfloat16).reshape(block_rows, heads_dev * HD)

    attended = lax.map(attend_block, jnp.arange(tok_grp // block_rows, dtype=jnp.int32))
    attended = attended.reshape(tok_grp, heads_dev * HD)
    attended_back = lax.all_to_all(attended, "mp", split_axis=0, concat_axis=1, tiled=True)
    hidden_state = (
        tokens_f + jnp.dot(attended_back, output_weight, preferred_element_type=jnp.float32)
    ).astype(jnp.bfloat16)
    hidden_f = hidden_state.astype(jnp.float32)
    mlp_in = rms_scale(hidden_f, mlp_gain).astype(jnp.bfloat16)
    mlp_group = lax.all_gather(mlp_in, "mp", axis=0, tiled=True)
    rows_dev = gate_rows.shape[0]
    block_width = gate_rows.shape[1] // (dp_count * mp_count)

    def arrange(weight_rows):
        shaped = weight_rows.astype(jnp.bfloat16).reshape(rows_dev, dp_count, mp_count, block_width)
        return jnp.transpose(shaped, (0, 2, 1, 3)).reshape(
            rows_dev, mp_count, dp_count * block_width
        )

    gate_piece, up_piece = (
        lax.all_to_all(arrange(gate_rows), "mp", split_axis=1, concat_axis=0, tiled=True),
        lax.all_to_all(arrange(up_rows), "mp", split_axis=1, concat_axis=0, tiled=True),
    )
    gate_piece = gate_piece.reshape(rows_dev * mp_count, dp_count * block_width)
    up_piece = up_piece.reshape(rows_dev * mp_count, dp_count * block_width)
    gate_block, up_block = (
        lax.all_gather(gate_piece, "dp", axis=0, tiled=True),
        lax.all_gather(up_piece, "dp", axis=0, tiled=True),
    )
    gate = jnp.dot(mlp_group, gate_block, preferred_element_type=jnp.float32)
    upper = jnp.dot(mlp_group, up_block, preferred_element_type=jnp.float32)
    activated = (jax.nn.silu(gate) * upper).astype(jnp.bfloat16)
    down_block = lax.all_gather(down_rows.astype(jnp.bfloat16), "dp", axis=0, tiled=True)
    mlp_sum = lax.psum_scatter(
        jnp.dot(activated, down_block, preferred_element_type=jnp.float32).astype(jnp.bfloat16),
        "mp",
        scatter_dimension=0,
        tiled=True,
    ).astype(jnp.float32)
    layer_out = (hidden_f + mlp_sum).astype(jnp.bfloat16)
    pages_dev = tok_dev // PAGE
    feature = 2 * KVH * HD
    cache_rows = jnp.concatenate(
        [keys.reshape(tok_dev, KVH * HD), values.reshape(tok_dev, KVH * HD)], axis=1
    )
    holders = page_table[:, 0]
    order = jnp.arange(pages_dev, dtype=jnp.int32)
    same_earlier = (holders[None, :] == holders[:, None]) & (order[None, :] < order[:, None])
    rank = jnp.sum(same_earlier.astype(jnp.int32), axis=1)
    target = holders * PAGE_MOST + rank
    slot_range = jnp.arange(dp_count * PAGE_MOST, dtype=jnp.int32)
    placing = (slot_range[:, None] == target[None, :]).astype(jnp.bfloat16)
    flat_pages = cache_rows.reshape(pages_dev, PAGE * feature)
    page_send = jnp.dot(placing, flat_pages, preferred_element_type=jnp.float32).astype(
        jnp.bfloat16
    )
    page_send = page_send.reshape(dp_count, PAGE_MOST, PAGE, feature)
    received = lax.all_to_all(page_send, "dp", split_axis=0, concat_axis=0, tiled=True)
    page_cache = received[None, None]
    return (layer_out, page_cache)


def solution(mesh):
    return jax.shard_map(
        on_device,
        mesh=mesh,
        in_specs=(
            P(("dp", "mp"), None),
            P(),
            P(),
            P(),
            P(),
            P(),
            P(("dp", "mp"), None),
            P(("dp", "mp"), None),
            P(("dp", "mp"), None),
            P("dp", None),
            P(("dp", "mp")),
            P(("dp", "mp"), None),
        ),
        out_specs=(P(("dp", "mp"), None), P("dp", "mp", None, None, None, None)),
        check_vma=False,
    )
```

profile of v0, /device:TPU:0, one launch (start us, length us, event | category | flops | bytes accessed | tf_op | source)
XLA Modules:
  0.0 441.5 jit_solution(11806712546734390694)
XLA Ops:
  8.5 5.6 %all-to-all-start = ((bf16[128,16,1]{0,2,1:T(2,128)(2,1)}), bf16[128,16,1]{0,2,1:T(2,128)(2,1)S(1)}, u32[]{:S(2)}, u32[]{:S(2)}) async-start(bf16[128,16,1]{0,2,1:T(2,128)(2,1)} %broadcast_in_dim.28), calls=%async_computation | async-start | bytes 16384 | tf_op jit(solution)/shard_map/all_to_all | solution.py:85
  15.4 3.1 fusion.40
  20.7 5.7 %all-to-all-start.4 = ((bf16[16,16,512]{2,0,1:T(8,128)(2,1)}), bf16[16,16,512]{2,0,1:T(8,128)(2,1)S(1)}, u32[]{:S(2)}, u32[]{:S(2)}) async-start(bf16[16,16,512]{2,0,1:T(8,128)(2,1)} %copy.77), calls=%async_computation.4 | async-start | bytes 524288 | tf_op jit(solution)/shard_map/all_to_all | solution.py:135
  26.7 7.8 %all-to-all-done.4 = bf16[16,16,512]{2,0,1:T(8,128)(2,1)S(1)} async-done(((bf16[16,16,512]{2,0,1:T(8,128)(2,1)}), bf16[16,16,512]{2,0,1:T(8,128)(2,1)S(1)}, u32[]{:S(2)}, u32[]{:S(2)}) %all-to-all-start.4) | async-done | bytes 262176 | tf_op jit(solution)/shard_map/all_to_all | solution.py:135
  35.4 3.6 all-to-all-start.2
  39.0 6.8 %fusion.42 = f32[128,2048]{0,1:T(8,128)S(1)} fusion(bf16[2048,2048]{1,0:T(8,128)(2,1)} %param.17, bf16[128,2048]{1,0:T(8,128)(2,1)S(1)} %copy-done, f32[2048]{0:T(1024)S(1)} %copy-done.6, f32[128]{0:T(128)S(1)} %add_rsqrt_fusion.1), kind=kOutput, calls=%fused_computation.57 | convolution fusion | flops 1074790400 | bytes 9970176 | tf_op jit(solution)/shard_map/dot_general | solution.py:72
  47.5 2.3 all-to-all-done.2
  49.8 3.6 all-to-all-start.1
  56.0 8.3 %all-to-all-done.1 = bf16[128,16,128]{0,2,1:T(8,128)(2,1)S(1)} async-done(((bf16[128,16,128]{0,2,1:T(8,128)(2,1)}), bf16[128,16,128]{0,2,1:T(8,128)(2,1)S(1)}, u32[]{:S(2)}, u32[]{:S(2)}) %all-to-all-start.1) | async-done | bytes 524320 | tf_op jit(solution)/shard_map/all_to_all | solution.py:83
  64.8 68.6 %while.12 = (s32[]{:T(128)}, bf16[4,512,128]{2,1,0:T(8,128)(2,1)S(1)}, s32[4]{0:T(128)S(1)}, s32[2048]{0:T(1024)S(1)}, pred[2048]{0:T(1024)(128)(4,1)S(1)}, /*in...) while((s32[]{:T(128)}, ...), condition=%wide.region_4.5_spmd.clone.clone, body=%wide.region_1.0_spmd.clone.clone.sunk | while | flops 555813376 | bytes 20213952 | solution.py:116
  66.2 3.6 fusion.77
  69.8 7.2 %fusion.78 = (f32[2,512]{1,0:T(2,128)S(1)}, f32[2,512,2048]{2,1,0:T(8,128)}) fusion(pred[512,2048]{1,0:T(8,128)(4,1)S(1)} %fusion.77, bf16[2048,64]{0,1:T(8,128)(2,1)} %get-tuple-element.220, bf16[2048,2,64]{0,2,1:T(8,128)(2,1)S(1)} %get-tuple-element.219, s32[]{:T(128)S(6)} %select_n.41), kind=kOutput, calls=%fused_computation.76.clone.1 | convolution fusion | flops 276826112 | bytes 9834500 | tf_op jit(solution)/shard_map/while/body/eval_jaxpr/sub | solution.py:111
  77.0 4.8 %fusion.79 = bf16[2,512,64]{1,2,0:T(8,128)(2,1)S(1)} fusion(f32[2,512,2048]{2,1,0:T(8,128)} %get-tuple-element.188, f32[2,512]{1,0:T(2,128)S(1)} %get-tuple-element.189, bf16[2048,64]{0,1:T(8,128)(2,1)S(1)} %get-tuple-element.221), kind=kOutput, calls=%fused_computation.17.clone.1 | convolution fusion | flops 272695296 | bytes 8785920 | tf_op jit(solution)/shard_map/while/body/eval_jaxpr/hts,sd->thd/dot_general | solution.py:113
  83.3 3.6 fusion.77
  87.0 7.2 %fusion.78 = (f32[2,512]{1,0:T(2,128)S(1)}, f32[2,512,2048]{2,1,0:T(8,128)}) fusion(pred[512,2048]{1,0:T(8,128)(4,1)S(1)} %fusion.77, bf16[2048,64]{0,1:T(8,128)(2,1)} %get-tuple-element.220, bf16[2048,2,64]{0,2,1:T(8,128)(2,1)S(1)} %get-tuple-element.219, s32[]{:T(128)S(6)} %select_n.41), kind=kOutput, calls=%fused_computation.76.clone.1 | convolution fusion | flops 276826112 | bytes 9834500 | tf_op jit(solution)/shard_map/while/body/eval_jaxpr/sub | solution.py:111
  94.2 4.9 %fusion.79 = bf16[2,512,64]{1,2,0:T(8,128)(2,1)S(1)} fusion(f32[2,512,2048]{2,1,0:T(8,128)} %get-tuple-element.188, f32[2,512]{1,0:T(2,128)S(1)} %get-tuple-element.189, bf16[2048,64]{0,1:T(8,128)(2,1)S(1)} %get-tuple-element.221), kind=kOutput, calls=%fused_computation.17.clone.1 | convolution fusion | flops 272695296 | bytes 8785920 | tf_op jit(solution)/shard_map/while/body/eval_jaxpr/hts,sd->thd/dot_general | solution.py:113
  100.5 3.6 fusion.77
  104.1 7.2 %fusion.78 = (f32[2,512]{1,0:T(2,128)S(1)}, f32[2,512,2048]{2,1,0:T(8,128)}) fusion(pred[512,2048]{1,0:T(8,128)(4,1)S(1)} %fusion.77, bf16[2048,64]{0,1:T(8,128)(2,1)} %get-tuple-element.220, bf16[2048,2,64]{0,2,1:T(8,128)(2,1)S(1)} %get-tuple-element.219, s32[]{:T(128)S(6)} %select_n.41), kind=kOutput, calls=%fused_computation.76.clone.1 | convolution fusion | flops 276826112 | bytes 9834500 | tf_op jit(solution)/shard_map/while/body/eval_jaxpr/sub | solution.py:111
  111.3 4.8 %fusion.79 = bf16[2,512,64]{1,2,0:T(8,128)(2,1)S(1)} fusion(f32[2,512,2048]{2,1,0:T(8,128)} %get-tuple-element.188, f32[2,512]{1,0:T(2,128)S(1)} %get-tuple-element.189, bf16[2048,64]{0,1:T(8,128)(2,1)S(1)} %get-tuple-element.221), kind=kOutput, calls=%fused_computation.17.clone.1 | convolution fusion | flops 272695296 | bytes 8785920 | tf_op jit(solution)/shard_map/while/body/eval_jaxpr/hts,sd->thd/dot_general | solution.py:113
  117.7 3.6 fusion.77
  121.3 7.2 %fusion.78 = (f32[2,512]{1,0:T(2,128)S(1)}, f32[2,512,2048]{2,1,0:T(8,128)}) fusion(pred[512,2048]{1,0:T(8,128)(4,1)S(1)} %fusion.77, bf16[2048,64]{0,1:T(8,128)(2,1)} %get-tuple-element.220, bf16[2048,2,64]{0,2,1:T(8,128)(2,1)S(1)} %get-tuple-element.219, s32[]{:T(128)S(6)} %select_n.41), kind=kOutput, calls=%fused_computation.76.clone.1 | convolution fusion | flops 276826112 | bytes 9834500 | tf_op jit(solution)/shard_map/while/body/eval_jaxpr/sub | solution.py:111
  128.5 4.8 %fusion.79 = bf16[2,512,64]{1,2,0:T(8,128)(2,1)S(1)} fusion(f32[2,512,2048]{2,1,0:T(8,128)} %get-tuple-element.188, f32[2,512]{1,0:T(2,128)S(1)} %get-tuple-element.189, bf16[2048,64]{0,1:T(8,128)(2,1)S(1)} %get-tuple-element.221), kind=kOutput, calls=%fused_computation.17.clone.1 | convolution fusion | flops 272695296 | bytes 8785920 | tf_op jit(solution)/shard_map/while/body/eval_jaxpr/hts,sd->thd/dot_general | solution.py:113
  133.5 13.5 %all_to_all.96 = bf16[16,128,128]{2,1,0:T(8,128)(2,1)S(1)} all-to-all(bf16[16,128,128]{2,1,0:T(8,128)(2,1)S(1)} %bitcast.125), channel_id=1, replica_groups=mesh['dp'=8,'mp'=16] {'mp'}, dimensions={0} | all-to-all | bytes 1048576 | tf_op jit(solution)/shard_map/all_to_all | solution.py:118
  147.3 4.8 %multiply_reduce_fusion = (f32[128]{0:T(128)S(1)}, f32[128,2048]{1,0:T(8,128)S(1)}) fusion(bf16[128,2048]{0,1:T(8,128)(2,1)S(1)} %bitcast.112, bf16[2048,2048]{1,0:T(8,128)(2,1)} %param.19, bf16[128,2048]{1,0:T(8,128)(2,1)S(1)} %copy-done), kind=kOutput, calls=%fused_computation.44 | convolution fusion | flops 1075314560 | bytes 10486272 | tf_op jit(solution)/shard_map/dot_general | solution.py:120
  155.2 11.5 %all_to_all.97 = bf16[16,16,512]{2,0,1:T(8,128)(2,1)} all-to-all(bf16[16,16,512]{2,0,1:T(8,128)(2,1)S(1)} %copy.79), channel_id=1, replica_groups=mesh['dp'=8,'mp'=16] {'mp'}, dimensions={1} | all-to-all | bytes 524288 | tf_op jit(solution)/shard_map/all_to_all | solution.py:136
  167.0 38.4 %all-gather.5.cloned.1.call-done = bf16[2048,2048]{1,0:T(8,128)(2,1)} async-done(((bf16[128,2048]{1,0:T(8,128)(2,1)}), bf16[2048,2048]{1,0:T(8,128)(2,1)}) %all-gather.5.cloned.1.call-update) | async-done | bytes 8388624 | tf_op jit(solution)/shard_map/all_gather | solution.py:124
  205.4 10.4 %fusion.57 = f32[2048,512]{1,0:T(8,128)} fusion(bf16[2048,2048]{1,0:T(8,128)(2,1)} %all-gather.5.cloned.1.call-done, bf16[2048,512]{1,0:T(8,128)(2,1)} %all-gather.7.cloned.1.call-done), kind=kOutput, calls=%fused_computation.77 | convolution fusion | flops 4294967296 | bytes 14680064 | tf_op jit(solution)/shard_map/dot_general | solution.py:144
  215.9 48.2 %all-gather.11.cloned.1.call-done = bf16[512,2048]{1,0:T(8,128)(2,1)} async-done(((bf16[64,2048]{1,0:T(8,128)(2,1)}), bf16[512,2048]{1,0:T(8,128)(2,1)}) %all-gather.11.cloned.1.call-update) | async-done | bytes 2097168 | tf_op jit(solution)/shard_map/all_gather | solution.py:147
  264.0 54.1 %all-gather.9.cloned.1.call-done = bf16[2048,512]{1,0:T(8,128)(2,1)} async-done(((bf16[256,512]{1,0:T(8,128)(2,1)}), bf16[2048,512]{1,0:T(8,128)(2,1)}) %all-gather.9.cloned.1.call-update) | async-done | bytes 2097168 | tf_op jit(solution)/shard_map/all_gather | solution.py:142
  318.2 15.2 %convolution_convert_fusion.1 = bf16[2048,2048]{1,0:T(8,128)(2,1)} fusion(bf16[512,2048]{1,0:T(8,128)(2,1)} %all-gather.11.cloned.1.call-done, f32[2048,512]{1,0:T(8,128)} %fusion.57, bf16[2048,2048]{1,0:T(8,128)(2,1)} %all-gather.5.cloned.1.call-done, bf16[2048,512]{1,0:T(8,128)(2,1)} %all-gather.9.cloned.1.call-done), kind=kOutput, calls=%fused_computation.32 | convolution fusion | flops 8600420352 | bytes 25165824 | tf_op jit(solution)/shard_map/dot_general | solution.py:149
  334.8 18.6 %all_to_all.98 = bf16[8,2,16,1024]{3,2,1,0:T(8,128)(2,1)S(1)} all-to-all(bf16[8,2,16,1024]{3,2,1,0:T(8,128)(2,1)S(1)} %bitcast.120), channel_id=1, replica_groups=mesh['dp'=8,'mp'=16] {'dp'}, dimensions={0} | all-to-all | bytes 1048576 | tf_op jit(solution)/shard_map/all_to_all | solution.py:172
  353.5 78.8 %reduce-scatter.2.cloned.1.call-done = bf16[128,2048]{1,0:T(8,128)(2,1)} async-done(((bf16[2048,2048]{1,0:T(8,128)(2,1)}), bf16[128,2048]{1,0:T(8,128)(2,1)}) %reduce-scatter.2.cloned.1.call-update) | async-done | bytes 524304 | tf_op jit(solution)/shard_map/reduce_scatter | solution.py:148
  (100 shorter events, 20.9 us)
Async XLA Ops:
  7.2 11.7 %copy-start.2 = (f32[16,8192]{1,0:T(8,128)S(1)}, f32[16,8192]{1,0:T(8,128)}, u32[]{:S(2)}) copy-start(f32[16,8192]{1,0:T(8,128)} %param.20) | copy-start | bytes 1572868
  8.5 12.2 %all-to-all-start = ((bf16[128,16,1]{0,2,1:T(2,128)(2,1)}), bf16[128,16,1]{0,2,1:T(2,128)(2,1)S(1)}, u32[]{:S(2)}, u32[]{:S(2)}) async-start(bf16[128,16,1]{0,2,1:T(2,128)(2,1)} %broadcast_in_dim.28), calls=%async_computation | async-start | bytes 16384 | tf_op jit(solution)/shard_map/all_to_all | solution.py:85
  18.7 20.3 %copy-start = (bf16[128,2048]{1,0:T(8,128)(2,1)S(1)}, bf16[128,2048]{1,0:T(8,128)(2,1)}, u32[]{:S(2)}) copy-start(bf16[128,2048]{1,0:T(8,128)(2,1)} %param.14) | copy-start | bytes 1572868
  18.7 20.3 %copy-start.6 = (f32[2048]{0:T(1024)S(1)}, f32[2048]{0:T(1024)}, u32[]{:S(2)}) copy-start(f32[2048]{0:T(1024)} %param.15) | copy-start | bytes 24580
  20.7 13.8 %all-to-all-start.4 = ((bf16[16,16,512]{2,0,1:T(8,128)(2,1)}), bf16[16,16,512]{2,0,1:T(8,128)(2,1)S(1)}, u32[]{:S(2)}, u32[]{:S(2)}) async-start(bf16[16,16,512]{2,0,1:T(8,128)(2,1)} %copy.77), calls=%async_computation.4 | async-start | bytes 524288 | tf_op jit(solution)/shard_map/all_to_all | solution.py:135
  34.5 11.3 %copy-start.1 = (bf16[16,16,512]{2,0,1:T(8,128)(2,1)}, bf16[16,16,512]{2,0,1:T(8,128)(2,1)S(1)}, u32[]{:S(2)}) copy-start(bf16[16,16,512]{2,0,1:T(8,128)(2,1)S(1)} %all-to-all-done.4) | copy-start | bytes 786436
  35.4 14.4 %all-to-all-start.2 = ((bf16[128,16,128]{0,2,1:T(8,128)(2,1)}), bf16[128,16,128]{0,2,1:T(8,128)(2,1)S(1)}, u32[]{:S(2)}, u32[]{:S(2)}) async-start(bf16[128,16,128]{0,2,1:T(8,128)(2,1)} %bitcast.10), calls=%async_computation.2 | async-start | bytes 1048576 | tf_op jit(solution)/shard_map/all_to_all | solution.py:84
  47.5 17.3 %copy-start.5 = (bf16[4,512,128]{2,1,0:T(8,128)(2,1)S(1)}, bf16[4,512,128]{2,1,0:T(8,128)(2,1)}, u32[]{:S(2)}) copy-start(bf16[4,512,128]{2,1,0:T(8,128)(2,1)} %custom-call) | copy-start | bytes 1572868
  49.8 14.4 %all-to-all-start.1 = ((bf16[128,16,128]{0,2,1:T(8,128)(2,1)}), bf16[128,16,128]{0,2,1:T(8,128)(2,1)S(1)}, u32[]{:S(2)}, u32[]{:S(2)}) async-start(bf16[128,16,128]{0,2,1:T(8,128)(2,1)} %bitcast.5), calls=%async_computation.1 | async-start | bytes 1048576 | tf_op jit(solution)/shard_map/all_to_all | solution.py:83
  53.4 113.6 %all-gather.7.cloned.1.call-start = ((), (), s32[]{:S(2)}) async-start(), calls=%async_computation.9 | async-start | bytes 2359296 | tf_op jit(solution)/shard_map/all_gather | solution.py:141
  54.1 151.3 %all-gather.5.cloned.1.call-start = ((), (), s32[]{:S(2)}) async-start(), calls=%async_computation.8 | async-start | bytes 8912896 | tf_op jit(solution)/shard_map/all_gather | solution.py:124
  147.3 4.9 %copy-start.7 = (f32[2048]{0:T(1024)S(1)}, f32[2048]{0:T(1024)}, u32[]{:S(2)}) copy-start(f32[2048]{0:T(1024)} %param.16) | copy-start | bytes 24580
  147.3 5.9 %copy-start.3 = (f32[64,2048]{1,0:T(8,128)S(1)}, f32[64,2048]{1,0:T(8,128)}, u32[]{:S(2)}) copy-start(f32[64,2048]{1,0:T(8,128)} %param.22) | copy-start | bytes 1572868
  147.3 6.7 %copy-start.4 = (f32[16,8192]{1,0:T(8,128)S(1)}, f32[16,8192]{1,0:T(8,128)}, u32[]{:S(2)}) copy-start(f32[16,8192]{1,0:T(8,128)} %param.21) | copy-start | bytes 1572868
  153.1 110.9 %all-gather.11.cloned.1.call-start = ((), (), s32[]{:S(2)}) async-start(), calls=%async_computation.11 | async-start | bytes 2359296 | tf_op jit(solution)/shard_map/all_gather | solution.py:147
  153.9 164.2 %all-gather.9.cloned.1.call-start = ((), (), s32[]{:S(2)}) async-start(), calls=%async_computation.10 | async-start | bytes 2359296 | tf_op jit(solution)/shard_map/all_gather | solution.py:142
  166.7 265.5 %reduce-scatter.2.cloned.1.call-start = ((), (), s32[]{:S(2)}) async-start(), calls=%async_computation.12 | async-start | bytes 8912896 | tf_op jit(solution)/shard_map/reduce_scatter | solution.py:148
  333.4 0.7 copy-start.8
Sparse Core Ops, SparseCore 0:
  56.6 56.3 all-gather.6
  153.2 52.1 all-gather.4
  208.4 55.6 all-gather.10
  266.2 51.8 all-gather.8
  333.6 98.6 reduce-scatter.1
where the time goes:
time: 443 us; the launch traced here: 441 us
  waiting for transfers between devices  239 us (54%)
  matrix products  88.7 us (20%)
  blocking collectives  43.6 us (10%)
  other arithmetic  21.6 us (5%)
  starting transfers between devices  19.1 us (4%)
  between operations  14.8 us (3%)
  local copies, waits for them, and re-layouts  12.2 us (3%)
    reduce_scatter x1, waiting for transfers between devices, on_device(): lax.psum_scatter(jnp.dot(activated, down_block, preferred_element_type=jn...  78.8 us
    all_gather x1, waiting for transfers between devices, on_device(): lax.all_gather(up_piece, 'dp', axis=0, tiled=True)  54.1 us
    all_gather x1, waiting for transfers between devices, on_device(): lax.all_gather(down_rows.astype(jnp.bfloat16), 'dp', axis=0, tiled=True)  48.2 us
    all_gather x1, waiting for transfers between devices, on_device(): mlp_group = lax.all_gather(mlp_in, 'mp', axis=0, tiled=True)  38.4 us
    sub x4, matrix products, attend_block(): expd = jnp.exp(scores - top)  28.7 us
    dot_general x4, matrix products, attend_block(): jnp.einsum('hts,sd->thd', weights, value_in, preferred_element_type=jnp.f...  19.4 us
    all_to_all x1, blocking collectives, on_device(): lax.all_to_all(page_send, 'dp', split_axis=0, concat_axis=0, tiled=True)  18.6 us
    dot_general x1, matrix products, on_device(): jnp.dot(activated, down_block, preferred_element_type=jnp.float32)  15.2 us
  transfers between devices with their start and end apart: 9, of which 7 were waited for; matrix products, arithmetic and copies ran while one was open for 23% of the time, Pallas kernels for 0%

commit v1 on v0

v1 whole, which is shorter than its diff:
```python
import functools
import math

import jax
import jax.numpy as jnp
from jax import lax
from jax.experimental import pallas as pl
from jax.experimental.pallas import tpu as pltpu
from jax.sharding import PartitionSpec as P

MESH = pl.DeviceIdType.MESH
BF = jnp.bfloat16
F32 = jnp.float32
NDP = 8
NMP = 16
TD = 128
D = 2048
HB = 1024
NEG = -1e30
ANY = pl.BlockSpec(memory_space=pl.ANY)
VM = pl.BlockSpec(memory_space=pltpu.VMEM)
SM = pl.BlockSpec(memory_space=pltpu.SMEM)
VLIM = 62 * 1024 * 1024


def place():
    dp = lax.axis_index("dp")
    mp = lax.axis_index("mp")
    return dp, mp, lax.div(mp, 2), lax.rem(mp, 2)


def greet(peers):
    barrier = pltpu.get_barrier_semaphore()
    for peer in peers:
        pl.semaphore_signal(barrier, inc=1, device_id=peer, device_id_type=MESH)
    return barrier, len(peers)


def send(src, dst, ssem, rsem, dev):
    copy = pltpu.make_async_remote_copy(
        src_ref=src, dst_ref=dst, send_sem=ssem, recv_sem=rsem, device_id=dev, device_id_type=MESH
    )
    return copy


def landed(dst, ssem, rsem, dev):
    send(dst, dst, ssem, rsem, dev).wait_recv()


def norm_rows(x, gain):
    ms = jnp.mean(x * x, axis=-1, keepdims=True)
    return x * lax.rsqrt(ms + 1e-05) * gain


def front(
    tok, gain, wq, wkv, gate, up, down, valid,
    qkv_in, flag_in, wg, wu, wd, kvrows,
    wv, normed, cs, sbuf, fbuf, gs, us, dbf, kbuf, vbuf,
    wsem, qs, qr, fs, fr, gsend, grecv, usend, urecv, lsem,
):
    dp, mp, chip, core = place()
    others = [lax.rem(mp + s, NMP) for s in range(1, NMP)]
    barrier, count = greet([{"mp": j} for j in others])
    wcopies = []
    for n in range(6):
        src = wkv.at[:, pl.ds((n - 4) * 512, 512)] if n >= 4 else wq.at[:, pl.ds(n * 512, 512)]
        wcopies.append(pltpu.make_async_copy(src, wv.at[n], wsem.at[n]))
    order = (4, 5, 0, 1, 2, 3)
    for n in order:
        wcopies[n].start()
    for c in range(8):
        for i in range(8):
            cols = slice((i * 8 + c) * 128, (i * 8 + c + 1) * 128)
            gs[c, :, i * 128 : (i + 1) * 128] = gate[:, cols].astype(BF)
            us[c, :, i * 128 : (i + 1) * 128] = up[:, cols].astype(BF)
    dbf[...] = down[...].astype(BF)
    fbuf[...] = jnp.broadcast_to(valid[...].astype(F32), (16, TD)).astype(BF)
    local = [
        pltpu.make_async_copy(gs.at[chip], wg.at[dp, chip, core], lsem.at[0]),
        pltpu.make_async_copy(us.at[chip], wu.at[dp, chip, core], lsem.at[1]),
        pltpu.make_async_copy(dbf, wd.at[dp, core], lsem.at[2]),
        pltpu.make_async_copy(fbuf, flag_in.at[mp], lsem.at[3]),
    ]
    for copy in local:
        copy.start()
    pl.semaphore_wait(barrier, count)
    started = []
    for s in range(1, 8):
        c = lax.rem(chip + s, 8)
        dev = {"mp": c * 2 + core}
        for buf, out, ss, rs in ((gs, wg, gsend, grecv), (us, wu, usend, urecv)):
            copy = send(buf.at[c], out.at[dp, chip, core], ss.at[s], rs.at[s], dev)
            copy.start()
            started.append(copy)
    for s in range(1, NMP):
        copy = send(fbuf, flag_in.at[mp], fs.at[s], fr.at[s], {"mp": others[s - 1]})
        copy.start()
        started.append(copy)

    x = tok[...].astype(F32)
    normed[...] = norm_rows(x, gain[...]).astype(BF)
    lane = lax.broadcasted_iota(jnp.int32, (TD, 128), 1)
    row = lax.broadcasted_iota(jnp.int32, (TD, 128), 0) + mp * TD
    pos = row.astype(F32)
    freq = jnp.exp(lax.rem(lane, 32).astype(F32) * (-(2.0 / 64.0) * math.log(500000.0)))
    angle = pos * freq
    cs[0] = jnp.cos(angle)
    cs[1] = jnp.sin(angle)
    low = lane < 64
    first = lax.rem(lane, 64) < 32

    def turn(t):
        after = pltpu.roll(t, 96, 1)
        before = pltpu.roll(t, 32, 1)
        return t * cs[0] + jnp.where(first, -after, before) * cs[1]

    for n in order:
        wcopies[n].wait()
        acc = jnp.dot(normed[...], wv[n], preferred_element_type=F32)
        for l in range(4):
            t = acc[:, l * 128 : (l + 1) * 128]
            if n == 4:
                t = turn(t)
                kbuf[:, l * 128 : (l + 1) * 128] = t
                kvrows[:, l * 128 : (l + 1) * 128] = t.astype(BF)
            elif n == 5:
                vbuf[:, l * 128 : (l + 1) * 128] = t
                kvrows[:, 512 + l * 128 : 512 + (l + 1) * 128] = t.astype(BF)
            else:
                sbuf[n * 4 + l, 0] = (turn(t) * (0.125 * math.log2(math.e))).astype(BF)
        if n == 5:
            for l in range(4):
                kt = kbuf[:, l * 128 : (l + 1) * 128]
                vt = vbuf[:, l * 128 : (l + 1) * 128]
                even = jnp.where(low, kt, pltpu.roll(vt, 64, 1)).astype(BF)
                odd = jnp.where(low, pltpu.roll(kt, 64, 1), vt).astype(BF)
                sbuf[4 * l, 1] = even
                sbuf[4 * l + 1, 1] = even
                sbuf[4 * l + 2, 1] = odd
                sbuf[4 * l + 3, 1] = odd
    own = pltpu.make_async_copy(sbuf.at[mp], qkv_in.at[mp], lsem.at[4])
    own.start()
    for s in range(1, NMP):
        j = others[s - 1]
        copy = send(sbuf.at[j], qkv_in.at[mp], qs.at[s], qr.at[s], {"mp": j})
        copy.start()
        started.append(copy)
    own.wait()
    for copy in local:
        copy.wait()
    for copy in started:
        copy.wait_send()
    for s in range(1, 8):
        c = lax.rem(chip + 8 - s, 8)
        dev = {"mp": c * 2 + core}
        landed(wg.at[dp, c, core], gsend.at[s], grecv.at[s], dev)
        landed(wu.at[dp, c, core], usend.at[s], urecv.at[s], dev)
    for s in range(1, NMP):
        j = lax.rem(mp + NMP - s, NMP)
        landed(flag_in.at[j], fs.at[s], fr.at[s], {"mp": j})
        landed(qkv_in.at[j], qs.at[s], qr.at[s], {"mp": j})


def run_front(tok, gain, wq, wkv, gate, up, down, valid):
    sds = jax.ShapeDtypeStruct
    dma = pltpu.SemaphoreType.DMA
    return pl.pallas_call(
        front,
        out_shape=(
            sds((NMP, 2, TD, 128), BF),
            sds((NMP, 16, TD), BF),
            sds((8, 8, 2, 16, HB), BF),
            sds((8, 8, 2, 16, HB), BF),
            sds((8, 2, 64, D), BF),
            sds((TD, 1024), BF),
        ),
        in_specs=[VM, VM, ANY, ANY, VM, VM, VM, VM],
        out_specs=(ANY, ANY, ANY, ANY, ANY, VM),
        scratch_shapes=[
            pltpu.VMEM((6, D, 512), BF),
            pltpu.VMEM((TD, D), BF),
            pltpu.VMEM((2, TD, 128), F32),
            pltpu.VMEM((NMP, 2, TD, 128), BF),
            pltpu.VMEM((16, TD), BF),
            pltpu.VMEM((8, 16, HB), BF),
            pltpu.VMEM((8, 16, HB), BF),
            pltpu.VMEM((64, D), BF),
            pltpu.VMEM((TD, 512), F32),
            pltpu.VMEM((TD, 512), F32),
            dma((6,)), dma((NMP,)), dma((NMP,)), dma((NMP,)), dma((NMP,)),
            dma((8,)), dma((8,)), dma((8,)), dma((8,)), dma((5,)),
        ],
        compiler_params=pltpu.CompilerParams(
            collective_id=1, has_side_effects=True, vmem_limit_bytes=VLIM
        ),
        name="front",
    )(tok, gain, wq, wkv, gate, up, down, valid)


class Relay:
    def __init__(self, wg, wu, wd, ssem, rsem):
        self.wg, self.wu, self.wd, self.ssem, self.rsem = wg, wu, wd, ssem, rsem
        dp, mp, chip, core = place()
        z, xh = lax.div(dp, 2), lax.rem(dp, 2)
        self.core, self.xh = core, xh
        self.zm, self.zp, self.z2, self.z = lax.rem(z + 3, 4), lax.rem(z + 1, 4), lax.rem(z + 2, 4), z
        self.xo = 1 - xh
        self.partner = {"mp": chip * 2 + 1 - core}
        self.up = {"dp": self.zp * 2 + xh}
        self.down = {"dp": self.zm * 2 + xh}
        self.across = {"dp": z * 2 + self.xo}
        self.count = 0
        self.started = []

    def part(self, block, core, p):
        if p == 0:
            return self.wg.at[block, :, core]
        if p == 1:
            return self.wu.at[block, :, core]
        if p == 2:
            return self.wd.at[block, core, pl.ds(0, 32)]
        return self.wd.at[block, core, pl.ds(32, 32)]

    def put(self, block, parts, event, dev):
        for p in parts:
            ref = self.part(block, self.core, p)
            copy = send(ref, ref, self.ssem.at[self.count], self.rsem.at[event, p], dev)
            copy.start()
            self.started.append(copy)
            self.count += 1

    def got(self, block, parts, event, core=None):
        for p in parts:
            ref = self.part(block, self.core if core is None else core, p)
            landed(ref, self.ssem.at[0], self.rsem.at[event, p], self.partner)

    def finish(self):
        for copy in self.started:
            copy.wait_send()

    def stage0(self):
        b = self.z * 2 + self.xh
        self.put(b, (0, 1, 2, 3), 0, self.across)
        self.put(b, (0, 1, 2, 3), 1, self.up)
        self.put(b, (0, 1, 2, 3), 2, self.down)
        self.put(b, (0, 1, 2, 3), 8, self.partner)

    def stage1(self):
        b = self.z * 2 + self.xo
        self.got(b, (0, 1, 2, 3), 0)
        self.put(b, (0, 1, 2, 3), 3, self.up)
        self.put(b, (0, 1, 2, 3), 4, self.down)
        self.put(b, (0, 1, 2, 3), 9, self.partner)

    def stage2(self):
        b = self.zm * 2 + self.xh
        self.got(b, (0, 1, 2, 3), 1)
        self.put(b, (0, 2), 5, self.up)
        self.put(b, (0, 1, 2, 3), 10, self.partner)
        b = self.zp * 2 + self.xh
        self.got(b, (0, 1, 2, 3), 2)
        self.put(b, (1, 3), 5, self.down)
        self.put(b, (0, 1, 2, 3), 11, self.partner)

    def stage3(self):
        b = self.zm * 2 + self.xo
        self.got(b, (0, 1, 2, 3), 3)
        self.put(b, (0, 2), 6, self.up)
        self.put(b, (0, 1, 2, 3), 12, self.partner)
        b = self.zp * 2 + self.xo
        self.got(b, (0, 1, 2, 3), 4)
        self.put(b, (1, 3), 6, self.down)
        self.put(b, (0, 1, 2, 3), 13, self.partner)

    def stage4(self):
        b = self.z2 * 2 + self.xh
        self.got(b, (0, 1, 2, 3), 5)
        self.put(b, (0, 1, 2, 3), 14, self.partner)
        b = self.z2 * 2 + self.xo
        self.got(b, (0, 1, 2, 3), 6)
        self.put(b, (0, 1, 2, 3), 15, self.partner)

    def stage5(self):
        blocks = (
            self.z * 2 + self.xh, self.z * 2 + self.xo, self.zm * 2 + self.xh, self.zp * 2 + self.xh,
            self.zm * 2 + self.xo, self.zp * 2 + self.xo, self.z2 * 2 + self.xh, self.z2 * 2 + self.xo,
        )
        for e, b in enumerate(blocks):
            self.got(b, (0, 1, 2, 3), 8 + e, 1 - self.core)


def attend(
    qkv, flags, kvrows, lens, table, wg_i, wu_i, wd_i,
    att_in, cache, wg, wu, wd,
    qa, ka, va, fb, tile, pbuf, m_s, acc_s,
    ssem, rsem, asend, arecv, psend, precv, lsem,
):
    dp, mp, chip, core = place()
    others = [lax.rem(mp + s, NMP) for s in range(1, NMP)]
    dothers = [lax.rem(dp + s, NDP) for s in range(1, NDP)]
    barrier, count = greet([{"mp": j} for j in others] + [{"dp": i} for i in dothers])
    relay = Relay(wg, wu, wd, ssem, rsem)
    length = lens[0, 0]

    holder = [table[p, 0] for p in range(8)]
    target = []
    for p in range(8):
        rank = jnp.int32(0)
        for q in range(p):
            rank = rank + jnp.where(holder[q] == holder[p], 1, 0)
        target.append(holder[p] * 2 + rank)
    col = lax.broadcasted_iota(jnp.int32, (256, 128), 1)
    row = lax.broadcasted_iota(jnp.int32, (256, 128), 0)
    want = jnp.zeros((256, 128), jnp.int32)
    for p in range(8):
        want = jnp.where(lax.div(col, 16) == p, target[p], want)
    pick = (lax.div(row, 16) == want) & (lax.rem(row, 16) == lax.rem(col, 16))
    pick = jnp.where(pick, 1.0, 0.0).astype(BF)
    pages = jnp.dot(pick, kvrows[...], preferred_element_type=F32).astype(BF)
    for i in range(8):
        for r in range(2):
            pbuf[i, r] = pages[(i * 2 + r) * 16 : (i * 2 + r + 1) * 16]

    pl.semaphore_wait(barrier, count)
    relay.stage0()
    started = []
    own_pages = pltpu.make_async_copy(pbuf.at[dp], cache.at[dp], lsem.at[0])
    own_pages.start()
    for s in range(1, NDP):
        i = dothers[s - 1]
        copy = send(pbuf.at[i], cache.at[dp], psend.at[s], precv.at[s], {"dp": i})
        copy.start()
        started.append(copy)

    lane = lax.broadcasted_iota(jnp.int32, (TD, 128), 1)
    sub = lax.broadcasted_iota(jnp.int32, (TD, 128), 0)
    low = lane < 64

    def prepare(b, carry):
        q = qkv[b, 0].astype(F32)
        kv = qkv[b, 1].astype(F32)
        frow = flags[b].astype(F32)[0:1, :]
        token = sub + b * TD
        late = jnp.where(token >= length, 1.0, 0.0)
        extra = jnp.where(lane == 64, 1.0, jnp.where(lane == 65, late, 0.0))
        qi, half = lax.div(b, 2), lax.rem(b, 2)
        qa[qi, pl.ds(half * TD, TD), :] = jnp.where(low, q, extra).astype(BF)
        qa[qi, pl.ds(256 + half * TD, TD), :] = jnp.where(low, pltpu.roll(q, 64, 1), extra).astype(BF)
        fcol = jnp.sum(jnp.where(lane == sub, frow, 0.0), axis=1, keepdims=True)
        closed = jnp.where(fcol > 0.5, 0.0, NEG)
        early = jnp.where(token >= length, 0.0, NEG)
        bias = jnp.where(lane == 64, closed, jnp.where(lane == 65, early, 0.0))
        ka[qi, pl.ds(half * TD, TD), :] = jnp.where(low, kv, bias).astype(BF)
        one = jnp.where(lane == 64, 1.0, 0.0)
        va[qi, pl.ds(half * TD, TD), :] = jnp.where(low, pltpu.roll(kv, 64, 1), one).astype(BF)
        fb[b] = jnp.broadcast_to(frow, (8, TD))
        return carry

    lax.fori_loop(0, NMP, prepare, 0)

    trow = lax.broadcasted_iota(jnp.int32, (512, 256), 0)
    trow = lax.rem(trow, 256)
    tcol = lax.broadcasted_iota(jnp.int32, (512, 256), 1)
    nt = (((1,), (1,)), ((), ()))
    qlane = lax.broadcasted_iota(jnp.int32, (512, 128), 1)
    hlane = lax.broadcasted_iota(jnp.int32, (256, 128), 1)

    def block(qi, carry):
        q = qa[qi]
        bare = jnp.where(qlane < 64, q.astype(F32), 0.0).astype(BF)
        s = lax.dot_general(bare, ka[qi], nt, preferred_element_type=F32)
        open_row = jnp.concatenate([fb[2 * qi][0:1], fb[2 * qi + 1][0:1]], axis=1) > 0.5
        base = qi * 256
        split = (trow + base >= length) & (tcol + base < length)
        ok = ((tcol < trow) & open_row & jnp.logical_not(split)) | (tcol == trow)
        s = jnp.where(ok, s, NEG)
        m = jnp.max(s, axis=1, keepdims=True)
        p = jnp.exp2(s - m)
        acc = jnp.dot(p.astype(BF), va[qi], preferred_element_type=F32)
        m_s[...] = m
        acc_s[...] = acc

        def step(ki, c2):
            s = lax.dot_general(qa[qi], ka[ki], nt, preferred_element_type=F32)
            m = m_s[...]
            m_new = jnp.maximum(m, jnp.max(s, axis=1, keepdims=True))
            p = jnp.exp2(s - m_new)
            acc_s[...] = acc_s[...] * jnp.exp2(m - m_new) + jnp.dot(
                p.astype(BF), va[ki], preferred_element_type=F32
            )
            m_s[...] = m_new
            return c2

        lax.fori_loop(0, qi, step, 0)
        acc = acc_s[...]
        out = acc / acc[:, 64:65]
        both = jnp.where(hlane < 64, out[:256], pltpu.roll(out[256:], 64, 1)).astype(BF)
        for half in range(2):
            j = 2 * qi + half
            tile[j] = both[half * TD : (half + 1) * TD]

            @pl.when(j != mp)
            def _():
                send(tile.at[j], att_in.at[mp], asend.at[j], arecv.at[mp], {"mp": j}).start()

            @pl.when(j == mp)
            def _():
                pltpu.make_async_copy(tile.at[j], att_in.at[j], lsem.at[1]).start()

        return carry

    lax.fori_loop(0, 4, block, 0)
    relay.stage1()
    lax.fori_loop(4, 8, block, 0)
    relay.stage2()
    relay.stage3()
    relay.stage4()
    relay.stage5()
    pltpu.make_async_copy(tile.at[mp], att_in.at[mp], lsem.at[1]).wait()
    for s in range(1, NMP):
        j = others[s - 1]
        copy = send(tile.at[j], att_in.at[j], asend.at[j], arecv.at[j], {"mp": j})
        copy.wait_send()
        copy.wait_recv()
    own_pages.wait()
    for s in range(1, NDP):
        started[s - 1].wait_send()
        i = lax.rem(dp + NDP - s, NDP)
        landed(cache.at[i], psend.at[s], precv.at[s], {"dp": i})
    relay.finish()


def run_attend(qkv, flags, kvrows, lens, table, wg, wu, wd):
    sds = jax.ShapeDtypeStruct
    dma = pltpu.SemaphoreType.DMA
    return pl.pallas_call(
        attend,
        out_shape=(
            sds((NMP, TD, 128), BF),
            sds((NDP, 2, 16, 1024), BF),
            sds(wg.shape, BF),
            sds(wu.shape, BF),
            sds(wd.shape, BF),
        ),
        in_specs=[VM, VM, VM, SM, SM, ANY, ANY, ANY],
        out_specs=(ANY, ANY, ANY, ANY, ANY),
        input_output_aliases={5: 2, 6: 3, 7: 4},
        scratch_shapes=[
            pltpu.VMEM((8, 512, 128), BF),
            pltpu.VMEM((8, 256, 128), BF),
            pltpu.VMEM((8, 256, 128), BF),
            pltpu.VMEM((NMP, 8, TD), F32),
            pltpu.VMEM((NMP, TD, 128), BF),
            pltpu.VMEM((NDP, 2, 16, 1024), BF),
            pltpu.VMEM((512, 1), F32),
            pltpu.VMEM((512, 128), F32),
            dma((72,)), dma((16, 4)), dma((NMP,)), dma((NMP,)), dma((NDP,)), dma((NDP,)), dma((2,)),
        ],
        compiler_params=pltpu.CompilerParams(
            collective_id=2, has_side_effects=True, vmem_limit_bytes=VLIM
        ),
        name="attend",
    )(qkv, flags, kvrows, lens, table, wg, wu, wd)


def mlp(
    att, tok, gain, wo, wg, wu, wd,
    out,
    att_v, wo_v, wg_v, wu_v, wd_v, hid, act, hbuf, part, rs,
    wsem, gs, gr, ss, sr,
):
    dp, mp, chip, core = place()
    y, x = lax.div(chip, 2), lax.rem(chip, 2)
    yp, ym, y2, xo = lax.rem(y + 1, 4), lax.rem(y + 3, 4), lax.rem(y + 2, 4), 1 - x

    def dev(yy, xx):
        return {"mp": (yy * 2 + xx) * 2 + core}

    peers = [(y, xo), (yp, x), (ym, x), (yp, xo), (ym, xo), (y2, x), (y2, xo)]
    barrier, count = greet([dev(*p) for p in peers])
    loads = [
        pltpu.make_async_copy(wo, wo_v, wsem.at[0]),
        pltpu.make_async_copy(wg, wg_v, wsem.at[1]),
        pltpu.make_async_copy(wu, wu_v, wsem.at[2]),
        pltpu.make_async_copy(wd, wd_v, wsem.at[3]),
    ]
    for copy in loads:
        copy.start()
    for j in range(NMP):
        att_v[:, j * 128 : (j + 1) * 128] = att[j]
    loads[0].wait()

    def project(n, carry):
        cols = pl.ds(pl.multiple_of(n * 512, 512), 512)
        got = jnp.dot(att_v[...], wo_v[:, cols], preferred_element_type=F32)
        hid[:, cols] = (tok[:, cols].astype(F32) + got).astype(BF).astype(F32)
        return carry

    lax.fori_loop(0, 4, project, 0)
    act[chip] = norm_rows(hid[...], gain[...]).astype(BF)
    pl.semaphore_wait(barrier, count)

    started = []
    half = (pl.ds(0, 64), pl.ds(64, 64))

    def forward(block, rows, event, to):
        ref = act.at[block] if rows is None else act.at[block, rows]
        copy = send(ref, ref, gs.at[len(started)], gr.at[event], dev(*to))
        copy.start()
        started.append(copy)

    def arrive(block, rows, event):
        ref = act.at[block] if rows is None else act.at[block, rows]
        landed(ref, gs.at[0], gr.at[event], dev(y, xo))

    def slot(yy, xx):
        return yy * 2 + xx

    mine = slot(y, x)
    forward(mine, None, 0, (y, xo))
    forward(mine, None, 1, (yp, x))
    forward(mine, None, 2, (ym, x))
    arrive(slot(y, xo), None, 0)
    forward(slot(y, xo), None, 3, (yp, x))
    forward(slot(y, xo), None, 4, (ym, x))
    arrive(slot(ym, x), None, 1)
    forward(slot(ym, x), half[0], 5, (yp, x))
    arrive(slot(yp, x), None, 2)
    forward(slot(yp, x), half[1], 6, (ym, x))
    for copy in loads[1:]:
        copy.wait()

    sends = []

    def pair(yy):
        rows = act.at[pl.ds(yy * 2, 2)]
        w_g = wg_v
        w_u = wu_v

        def hidden(n, carry):
            cols = pl.ds(pl.multiple_of(n * 256, 256), 256)
            xin = rows[...].reshape(256, D)
            g = jnp.dot(xin, w_g[:, cols], preferred_element_type=F32)
            u = jnp.dot(xin, w_u[:, cols], preferred_element_type=F32)
            hbuf[:, cols] = (g / (1.0 + jnp.exp(-g)) * u).astype(BF)
            return carry

        lax.fori_loop(0, 4, hidden, 0)

        def final(n, carry):
            cols = pl.ds(pl.multiple_of(n * 512, 512), 512)
            r = jnp.dot(hbuf[...], wd_v[:, cols], preferred_element_type=F32).astype(BF)
            part[yy * 2, :, cols] = r[:TD]
            part[yy * 2 + 1, :, cols] = r[TD:]
            return carry

        lax.fori_loop(0, 4, final, 0)

    def give(yy, xx, event):
        copy = send(part.at[slot(yy, xx)], rs.at[mine], ss.at[event], sr.at[event], dev(yy, xx))
        copy.start()
        sends.append(copy)

    pair(y)
    give(y, xo, 0)
    arrive(slot(ym, xo), None, 3)
    forward(slot(ym, xo), half[0], 7, (yp, x))
    arrive(slot(yp, xo), None, 4)
    forward(slot(yp, xo), half[1], 8, (ym, x))
    pair(ym)
    give(ym, x, 1)
    give(ym, xo, 2)
    pair(yp)
    give(yp, x, 3)
    give(yp, xo, 4)
    arrive(slot(y2, x), half[0], 5)
    arrive(slot(y2, x), half[1], 6)
    arrive(slot(y2, xo), half[0], 7)
    arrive(slot(y2, xo), half[1], 8)
    pair(y2)
    give(y2, x, 5)
    give(y2, xo, 6)
    for event, src in enumerate([(y, xo), (yp, x), (yp, xo), (ym, x), (ym, xo), (y2, x), (y2, xo)]):
        landed(rs.at[slot(*src)], ss.at[event], sr.at[event], dev(*src))
    rs[mine] = part[mine]

    def close(n, carry):
        cols = pl.ds(pl.multiple_of(n * 256, 256), 256)
        total = rs[0, :, cols].astype(F32)
        for c in range(1, 8):
            total = total + rs[c, :, cols].astype(F32)
        out[:, cols] = (hid[:, cols] + total).astype(BF)
        return carry

    lax.fori_loop(0, 8, close, 0)
    for copy in started + sends:
        copy.wait_send()


def run_mlp(att, tok, gain, wo, wg, wu, wd):
    dma = pltpu.SemaphoreType.DMA
    return pl.pallas_call(
        mlp,
        out_shape=jax.ShapeDtypeStruct((TD, D), BF),
        in_specs=[VM, VM, VM, ANY, ANY, ANY, ANY],
        out_specs=VM,
        scratch_shapes=[
            pltpu.VMEM((TD, D), BF),
            pltpu.VMEM((D, D), BF),
            pltpu.VMEM((D, HB), BF),
            pltpu.VMEM((D, HB), BF),
            pltpu.VMEM((HB, D), BF),
            pltpu.VMEM((TD, D), F32),
            pltpu.VMEM((8, TD, D), BF),
            pltpu.VMEM((256, HB), BF),
            pltpu.VMEM((8, TD, D), BF),
            pltpu.VMEM((8, TD, D), BF),
            dma((4,)), dma((9,)), dma((9,)), dma((7,)), dma((7,)),
        ],
        compiler_params=pltpu.CompilerParams(
            collective_id=3, has_side_effects=True, vmem_limit_bytes=VLIM
        ),
        name="mlp",
    )(att, tok, gain, wo, wg, wu, wd)


def on_device(
    tokens, attn_gain, mlp_gain, query_weight, keyval_weight, output_weight,
    gate_rows, up_rows, down_rows, lengths, valid, page_table,
):
    qkv, flags, wg, wu, wd, kvrows = run_front(
        tokens, attn_gain.reshape(1, D), query_weight, keyval_weight,
        gate_rows, up_rows, down_rows, valid.reshape(1, TD),
    )
    att, cache, wg, wu, wd = run_attend(qkv, flags, kvrows, lengths, page_table, wg, wu, wd)
    layer_out = run_mlp(
        att, tokens, mlp_gain.reshape(1, D), output_weight,
        wg.reshape(D, HB), wu.reshape(D, HB), wd.reshape(HB, D),
    )
    return (layer_out, cache[None, None])


def solution(mesh):
    return jax.shard_map(
        on_device,
        mesh=mesh,
        in_specs=(
            P(("dp", "mp"), None), P(), P(), P(), P(), P(),
            P(("dp", "mp"), None), P(("dp", "mp"), None), P(("dp", "mp"), None),
            P("dp", None), P(("dp", "mp")), P(("dp", "mp"), None),
        ),
        out_specs=(P(("dp", "mp"), None), P("dp", "mp", None, None, None, None)),
        check_vma=False,
    )
```

time: 443 us -> 198 us (0.45)
  waiting for transfers between devices: 239 us -> 0 us
  Pallas kernels: 0 us -> 193 us
  matrix products: 88.7 us -> 0 us
  blocking collectives: 43.6 us -> 0 us
  other arithmetic: 21.6 us -> 0 us
  starting transfers between devices: 19.1 us -> 0 us
  between operations: 14.8 us -> 1.31 us
  local copies, waits for them, and re-layouts: 12.2 us -> 4 us
    pallas_call x0 -> x3, Pallas kernels: none -> 193 us  [the longest x1 92 us: run_mlp(): pl.pallas_call(mlp, out_shape=jax.ShapeDtypeStruct((TD, D), BF), in_specs...]
    all_gather x4 -> x0, waiting for transfers between devices: 141 us -> none  [the longest x1 54.1 us: on_device(): lax.all_gather(up_piece, 'dp', axis=0, tiled=True)]
    reduce_scatter x1 -> x0, waiting for transfers between devices: 78.8 us -> none  [on_device(): lax.psum_scatter(jnp.dot(activated, down_block, preferred_element_type=jn...]
    dot_general x10 -> x0, matrix products: 60 us -> none  [the longest x4 19.4 us: attend_block(): jnp.einsum('hts,sd->thd', weights, value_in, preferred_element_type=jnp.f...]
    all_to_all x3 -> x0, blocking collectives: 43.6 us -> none  [the longest x1 18.6 us: on_device(): lax.all_to_all(page_send, 'dp', split_axis=0, concat_axis=0, tiled=True)]
    sub x4 -> x0, matrix products: 28.7 us -> none  [attend_block(): expd = jnp.exp(scores - top)]
    all_to_all x4 -> x0, starting transfers between devices: 18.4 us -> none  [the longest x1 5.72 us: on_device(): lax.all_to_all(arrange(gate_rows), 'mp', split_axis=1, concat_axis=0, til...]
    all_to_all x4 -> x0, waiting for transfers between devices: 18.4 us -> none  [the longest x1 8.26 us: on_device(): lax.all_to_all(query_send, 'mp', split_axis=1, concat_axis=0, tiled=True)]
  transfers between devices with their start and end apart: 9 -> 0, of which waited for: 7 -> 0; matrix products, arithmetic and copies ran while one was open for 23% -> 0% of each run, Pallas kernels for 0% -> 0%
where the time goes in v1:
time: 198 us
  Pallas kernels  193 us (97%)
  local copies, waits for them, and re-layouts  4 us (2%)
    pallas_call x1, Pallas kernels, run_mlp(): pl.pallas_call(mlp, out_shape=jax.ShapeDtypeStruct((TD, D), BF), in_specs...  92 us
    pallas_call x1, Pallas kernels, run_attend(): pl.pallas_call(attend, out_shape=(sds((NMP, TD, 128), BF), sds((NDP, 2, 1...  74.2 us
    pallas_call x1, Pallas kernels, run_front(): pl.pallas_call(front, out_shape=(sds((NMP, 2, TD, 128), BF), sds((NMP, 16...  26.5 us
    unnamed x5, local copies, waits for them, and re-layouts  4 us

profile of v1, /device:TPU:0, one launch (start us, length us, event | category | flops | bytes accessed | tf_op | source)
XLA Modules:
  0.0 198.0 jit_solution(9759927824919713861)
XLA Ops:
  1.3 1.3 copy.17.table
  2.6 26.5 %front.1 = (bf16[16,2,128,128]{3,2,1,0:T(8,128)(2,1)}, bf16[16,16,128]{2,1,0:T(8,128)(2,1)}, bf16[8,8,2,16,1024]{4,3,2,1,0:T(8,128)(2,1)}, bf16[8,8,2,16,1024]{4...) custom-call(bf16[128,2048]{1,0:T(8,128)(2,1)} %tok.3, f32[1,2048]{1,0:T(1,128)} %bitcast.12, ...), custom_call_target="tpu_custom_call" | custom-call | tf_op jit(solution)/shard_map/front/pallas_call | solution.py:167
  29.1 74.2 %attend.1 = (bf16[16,128,128]{2,1,0:T(8,128)(2,1)}, bf16[8,2,16,1024]{3,2,1,0:T(8,128)(2,1)}, bf16[8,8,2,16,1024]{4,3,2,1,0:T(8,128)(2,1)}, bf16[8,8,2,16,1024]{4,3,2,1,0:T(8,128)(2,1)}, bf16[8,2,64,2048]{3,2,1,0:T(8,128)(2,1)}) custom-call(bf16[16,2,128,128]{3,2,1,0:T(8,128)(2,1)} %get-tuple-element.13.qk, ...), custom_call_target="tpu_custom_call", output_to_operand_aliasing={{2}: (5, {}), {3}: (6, {}), {4}: (7, {})} | custom-call | tf_op jit(solution)/shard_map/attend/pallas_call | solution.py:436
  103.4 0.0 copy-start
  103.4 92.0 %mlp.1 = bf16[128,2048]{1,0:T(8,128)(2,1)} custom-call(bf16[16,128,128]{2,1,0:T(8,128)(2,1)} %get-tuple-element.19.att, bf16[128,2048]{1,0:T(8,128)(2,1)} %tok.3, f32[1,2048]{1,0:T(1,128)} %bitcast.11, bf16[2048,2048]{1,0:T(8,128)(2,1)} %wo.1, bf16[2048,1024]{1,0:T(8,128)(2,1)} %bitcast.7, bf16[2048,1024]{1,0:T(8,128)(2,1)} %bitcast.8, ...), custom_call_target="tpu_custom_call" | custom-call | tf_op jit(solution)/shard_map/mlp/pallas_call | solution.py:602
  195.3 1.9 copy.24
  197.2 0.0 copy-done
  197.2 0.8 copy.25
Async XLA Ops:
  103.4 93.9 %copy-start = (bf16[8,2,16,1024]{3,2,1,0:T(8,128)(2,1)S(1)}, bf16[8,2,16,1024]{3,2,1,0:T(8,128)(2,1)}, u32[]{:S(2)}) copy-start(bf16[8,2,16,1024]{3,2,1,0:T(8,128)(2,1)} %get-tuple-element.23) | copy-start | bytes 1572868

commit v2 on v1

--- a/solution.py
+++ b/solution.py
@@ -55,7 +55,7 @@
 def front(
     tok, gain, wq, wkv, gate, up, down, valid,
     qkv_in, flag_in, wg, wu, wd, kvrows,
-    wv, normed, cs, sbuf, fbuf, gs, us, dbf, kbuf, vbuf,
+    wv, normed, cs, sbuf, fbuf, gs, us, kbuf, vbuf,
     wsem, qs, qr, fs, fr, gsend, grecv, usend, urecv, lsem,
 ):
     dp, mp, chip, core = place()
@@ -73,13 +73,12 @@
             cols = slice((i * 8 + c) * 128, (i * 8 + c + 1) * 128)
             gs[c, :, i * 128 : (i + 1) * 128] = gate[:, cols].astype(BF)
             us[c, :, i * 128 : (i + 1) * 128] = up[:, cols].astype(BF)
-    dbf[...] = down[...].astype(BF)
+    wd[...] = down[...].astype(BF)
     fbuf[...] = jnp.broadcast_to(valid[...].astype(F32), (16, TD)).astype(BF)
     local = [
         pltpu.make_async_copy(gs.at[chip], wg.at[dp, chip, core], lsem.at[0]),
         pltpu.make_async_copy(us.at[chip], wu.at[dp, chip, core], lsem.at[1]),
-        pltpu.make_async_copy(dbf, wd.at[dp, core], lsem.at[2]),
-        pltpu.make_async_copy(fbuf, flag_in.at[mp], lsem.at[3]),
+        pltpu.make_async_copy(fbuf, flag_in.at[mp], lsem.at[2]),
     ]
     for copy in local:
         copy.start()
@@ -138,7 +137,7 @@
                 sbuf[4 * l + 1, 1] = even
                 sbuf[4 * l + 2, 1] = odd
                 sbuf[4 * l + 3, 1] = odd
-    own = pltpu.make_async_copy(sbuf.at[mp], qkv_in.at[mp], lsem.at[4])
+    own = pltpu.make_async_copy(sbuf.at[mp], qkv_in.at[mp], lsem.at[3])
     own.start()
     for s in range(1, NMP):
         j = others[s - 1]
@@ -171,11 +170,11 @@
             sds((NMP, 16, TD), BF),
             sds((8, 8, 2, 16, HB), BF),
             sds((8, 8, 2, 16, HB), BF),
-            sds((8, 2, 64, D), BF),
+            sds((64, D), BF),
             sds((TD, 1024), BF),
         ),
         in_specs=[VM, VM, ANY, ANY, VM, VM, VM, VM],
-        out_specs=(ANY, ANY, ANY, ANY, ANY, VM),
+        out_specs=(ANY, ANY, ANY, ANY, VM, VM),
         scratch_shapes=[
             pltpu.VMEM((6, D, 512), BF),
             pltpu.VMEM((TD, D), BF),
@@ -184,11 +183,10 @@
             pltpu.VMEM((16, TD), BF),
             pltpu.VMEM((8, 16, HB), BF),
             pltpu.VMEM((8, 16, HB), BF),
-            pltpu.VMEM((64, D), BF),
             pltpu.VMEM((TD, 512), F32),
             pltpu.VMEM((TD, 512), F32),
             dma((6,)), dma((NMP,)), dma((NMP,)), dma((NMP,)), dma((NMP,)),
-            dma((8,)), dma((8,)), dma((8,)), dma((8,)), dma((5,)),
+            dma((8,)), dma((8,)), dma((8,)), dma((8,)), dma((4,)),
         ],
         compiler_params=pltpu.CompilerParams(
             collective_id=1, has_side_effects=True, vmem_limit_bytes=VLIM
@@ -198,8 +196,8 @@
 
 
 class Relay:
-    def __init__(self, wg, wu, wd, ssem, rsem):
-        self.wg, self.wu, self.wd, self.ssem, self.rsem = wg, wu, wd, ssem, rsem
+    def __init__(self, part, ssem, rsem):
+        self.part, self.ssem, self.rsem = part, ssem, rsem
         dp, mp, chip, core = place()
         z, xh = lax.div(dp, 2), lax.rem(dp, 2)
         self.core, self.xh = core, xh
@@ -212,15 +210,6 @@
         self.count = 0
         self.started = []
 
-    def part(self, block, core, p):
-        if p == 0:
-            return self.wg.at[block, :, core]
-        if p == 1:
-            return self.wu.at[block, :, core]
-        if p == 2:
-            return self.wd.at[block, core, pl.ds(0, 32)]
-        return self.wd.at[block, core, pl.ds(32, 32)]
-
     def put(self, block, parts, event, dev):
         for p in parts:
             ref = self.part(block, self.core, p)
@@ -240,45 +229,45 @@
 
     def stage0(self):
         b = self.z * 2 + self.xh
-        self.put(b, (0, 1, 2, 3), 0, self.across)
-        self.put(b, (0, 1, 2, 3), 1, self.up)
-        self.put(b, (0, 1, 2, 3), 2, self.down)
-        self.put(b, (0, 1, 2, 3), 8, self.partner)
+        self.put(b, (0, 1), 0, self.across)
+        self.put(b, (0, 1), 1, self.up)
+        self.put(b, (0, 1), 2, self.down)
+        self.put(b, (0, 1), 8, self.partner)
 
     def stage1(self):
         b = self.z * 2 + self.xo
-        self.got(b, (0, 1, 2, 3), 0)
-        self.put(b, (0, 1, 2, 3), 3, self.up)
-        self.put(b, (0, 1, 2, 3), 4, self.down)
-        self.put(b, (0, 1, 2, 3), 9, self.partner)
+        self.got(b, (0, 1), 0)
+        self.put(b, (0, 1), 3, self.up)
+        self.put(b, (0, 1), 4, self.down)
+        self.put(b, (0, 1), 9, self.partner)
 
     def stage2(self):
         b = self.zm * 2 + self.xh
-        self.got(b, (0, 1, 2, 3), 1)
-        self.put(b, (0, 2), 5, self.up)
-        self.put(b, (0, 1, 2, 3), 10, self.partner)
+        self.got(b, (0, 1), 1)
+        self.put(b, (0,), 5, self.up)
+        self.put(b, (0, 1), 10, self.partner)
         b = self.zp * 2 + self.xh
-        self.got(b, (0, 1, 2, 3), 2)
-        self.put(b, (1, 3), 5, self.down)
-        self.put(b, (0, 1, 2, 3), 11, self.partner)
+        self.got(b, (0, 1), 2)
+        self.put(b, (1,), 5, self.down)
+        self.put(b, (0, 1), 11, self.partner)
 
     def stage3(self):
         b = self.zm * 2 + self.xo
-        self.got(b, (0, 1, 2, 3), 3)
-        self.put(b, (0, 2), 6, self.up)
-        self.put(b, (0, 1, 2, 3), 12, self.partner)
+        self.got(b, (0, 1), 3)
+        self.put(b, (0,), 6, self.up)
+        self.put(b, (0, 1), 12, self.partner)
         b = self.zp * 2 + self.xo
-        self.got(b, (0, 1, 2, 3), 4)
-        self.put(b, (1, 3), 6, self.down)
-        self.put(b, (0, 1, 2, 3), 13, self.partner)
+        self.got(b, (0, 1), 4)
+        self.put(b, (1,), 6, self.down)
+        self.put(b, (0, 1), 13, self.partner)
 
     def stage4(self):
         b = self.z2 * 2 + self.xh
-        self.got(b, (0, 1, 2, 3), 5)
-        self.put(b, (0, 1, 2, 3), 14, self.partner)
+        self.got(b, (0, 1), 5)
+        self.put(b, (0, 1), 14, self.partner)
         b = self.z2 * 2 + self.xo
-        self.got(b, (0, 1, 2, 3), 6)
-        self.put(b, (0, 1, 2, 3), 15, self.partner)
+        self.got(b, (0, 1), 6)
+        self.put(b, (0, 1), 15, self.partner)
 
     def stage5(self):
         blocks = (
@@ -286,12 +275,12 @@
             self.zm * 2 + self.xo, self.zp * 2 + self.xo, self.z2 * 2 + self.xh, self.z2 * 2 + self.xo,
         )
         for e, b in enumerate(blocks):
-            self.got(b, (0, 1, 2, 3), 8 + e, 1 - self.core)
+            self.got(b, (0, 1), 8 + e, 1 - self.core)
 
 
 def attend(
-    qkv, flags, kvrows, lens, table, wg_i, wu_i, wd_i,
-    att_in, cache, wg, wu, wd,
+    qkv, flags, kvrows, lens, table, wg_i, wu_i,
+    att_in, cache, wg, wu,
     qa, ka, va, fb, tile, pbuf, m_s, acc_s,
     ssem, rsem, asend, arecv, psend, precv, lsem,
 ):
@@ -299,7 +288,7 @@
     others = [lax.rem(mp + s, NMP) for s in range(1, NMP)]
     dothers = [lax.rem(dp + s, NDP) for s in range(1, NDP)]
     barrier, count = greet([{"mp": j} for j in others] + [{"dp": i} for i in dothers])
-    relay = Relay(wg, wu, wd, ssem, rsem)
+    relay = Relay(lambda b, c, p: (wg, wu)[p].at[b, :, c], ssem, rsem)
     length = lens[0, 0]
 
     holder = [table[p, 0] for p in range(8)]
@@ -410,10 +399,12 @@
         return carry
 
     lax.fori_loop(0, 4, block, 0)
+    relay.stage2()
+    lax.fori_loop(4, 5, block, 0)
     relay.stage1()
-    lax.fori_loop(4, 8, block, 0)
-    relay.stage2()
+    lax.fori_loop(5, 7, block, 0)
     relay.stage3()
+    lax.fori_loop(7, 8, block, 0)
     relay.stage4()
     relay.stage5()
     pltpu.make_async_copy(tile.at[mp], att_in.at[mp], lsem.at[1]).wait()
@@ -430,7 +421,7 @@
     relay.finish()
 
 
-def run_attend(qkv, flags, kvrows, lens, table, wg, wu, wd):
+def run_attend(qkv, flags, kvrows, lens, table, wg, wu):
     sds = jax.ShapeDtypeStruct
     dma = pltpu.SemaphoreType.DMA
     return pl.pallas_call(
@@ -440,11 +431,10 @@
             sds((NDP, 2, 16, 1024), BF),
             sds(wg.shape, BF),
             sds(wu.shape, BF),
-            sds(wd.shape, BF),
         ),
-        in_specs=[VM, VM, VM, SM, SM, ANY, ANY, ANY],
-        out_specs=(ANY, ANY, ANY, ANY, ANY),
-        input_output_aliases={5: 2, 6: 3, 7: 4},
+        in_specs=[VM, VM, VM, SM, SM, ANY, ANY],
+        out_specs=(ANY, ANY, ANY, ANY),
+        input_output_aliases={5: 2, 6: 3},
         scratch_shapes=[
             pltpu.VMEM((8, 512, 128), BF),
             pltpu.VMEM((8, 256, 128), BF),
@@ -454,20 +444,20 @@
             pltpu.VMEM((NDP, 2, 16, 1024), BF),
             pltpu.VMEM((512, 1), F32),
             pltpu.VMEM((512, 128), F32),
-            dma((72,)), dma((16, 4)), dma((NMP,)), dma((NMP,)), dma((NDP,)), dma((NDP,)), dma((2,)),
+            dma((30,)), dma((16, 2)), dma((NMP,)), dma((NMP,)), dma((NDP,)), dma((NDP,)), dma((2,)),
         ],
         compiler_params=pltpu.CompilerParams(
             collective_id=2, has_side_effects=True, vmem_limit_bytes=VLIM
         ),
         name="attend",
-    )(qkv, flags, kvrows, lens, table, wg, wu, wd)
+    )(qkv, flags, kvrows, lens, table, wg, wu)
 
 
 def mlp(
     att, tok, gain, wo, wg, wu, wd,
     out,
-    att_v, wo_v, wg_v, wu_v, wd_v, hid, act, hbuf, part, rs,
-    wsem, gs, gr, ss, sr,
+    att_v, wo_v, wg_v, wu_v, wd_v, hid, act, hbuf, part, rs, via,
+    wsem, gs, gr, ss, sr, wss, wsr,
 ):
     dp, mp, chip, core = place()
     y, x = lax.div(chip, 2), lax.rem(chip, 2)
@@ -477,15 +467,20 @@
         return {"mp": (yy * 2 + xx) * 2 + core}
 
     peers = [(y, xo), (yp, x), (ym, x), (yp, xo), (ym, xo), (y2, x), (y2, xo)]
-    barrier, count = greet([dev(*p) for p in peers])
+    relay = Relay(lambda b, c, p: wd_v.at[b, c, pl.ds(p * 32, 32)], wss, wsr)
+    barrier, count = greet([dev(*p) for p in peers] + [relay.partner, relay.up, relay.down, relay.across])
     loads = [
         pltpu.make_async_copy(wo, wo_v, wsem.at[0]),
         pltpu.make_async_copy(wg, wg_v, wsem.at[1]),
         pltpu.make_async_copy(wu, wu_v, wsem.at[2]),
-        pltpu.make_async_copy(wd, wd_v, wsem.at[3]),
+        pltpu.make_async_copy(wd, wd_v.at[dp, core], wsem.at[3]),
     ]
-    for copy in loads:
+    loads[3].start()
+    for copy in loads[:3]:
         copy.start()
+    pl.semaphore_wait(barrier, count)
+    loads[3].wait()
+    relay.stage0()
     for j in range(NMP):
         att_v[:, j * 128 : (j + 1) * 128] = att[j]
     loads[0].wait()
@@ -498,7 +493,6 @@
 
     lax.fori_loop(0, 4, project, 0)
     act[chip] = norm_rows(hid[...], gain[...]).astype(BF)
-    pl.semaphore_wait(barrier, count)
 
     started = []
     half = (pl.ds(0, 64), pl.ds(64, 64))
@@ -520,6 +514,8 @@
     forward(mine, None, 0, (y, xo))
     forward(mine, None, 1, (yp, x))
     forward(mine, None, 2, (ym, x))
+    relay.stage2()
+    relay.stage1()
     arrive(slot(y, xo), None, 0)
     forward(slot(y, xo), None, 3, (yp, x))
     forward(slot(y, xo), None, 4, (ym, x))
@@ -527,67 +523,92 @@
     forward(slot(ym, x), half[0], 5, (yp, x))
     arrive(slot(yp, x), None, 2)
     forward(slot(yp, x), half[1], 6, (ym, x))
-    for copy in loads[1:]:
+    relay.stage3()
+    for copy in loads[1:3]:
         copy.wait()
 
-    sends = []
-
-    def pair(yy):
+    def widen(k, yy):
         rows = act.at[pl.ds(yy * 2, 2)]
-        w_g = wg_v
-        w_u = wu_v
 
         def hidden(n, carry):
             cols = pl.ds(pl.multiple_of(n * 256, 256), 256)
             xin = rows[...].reshape(256, D)
-            g = jnp.dot(xin, w_g[:, cols], preferred_element_type=F32)
-            u = jnp.dot(xin, w_u[:, cols], preferred_element_type=F32)
-            hbuf[:, cols] = (g / (1.0 + jnp.exp(-g)) * u).astype(BF)
+            g = jnp.dot(xin, wg_v[:, cols], preferred_element_type=F32)
+            u = jnp.dot(xin, wu_v[:, cols], preferred_element_type=F32)
+            hbuf[k, :, cols] = (g / (1.0 + jnp.exp(-g)) * u).astype(BF)
             return carry
 
         lax.fori_loop(0, 4, hidden, 0)
 
+    def narrow(k, yy):
         def final(n, carry):
             cols = pl.ds(pl.multiple_of(n * 512, 512), 512)
-            r = jnp.dot(hbuf[...], wd_v[:, cols], preferred_element_type=F32).astype(BF)
+            w = wd_v[:, :, :, cols].reshape(HB, 512)
+            r = jnp.dot(hbuf[k], w, preferred_element_type=F32).astype(BF)
             part[yy * 2, :, cols] = r[:TD]
             part[yy * 2 + 1, :, cols] = r[TD:]
             return carry
 
         lax.fori_loop(0, 4, final, 0)
 
-    def give(yy, xx, event):
-        copy = send(part.at[slot(yy, xx)], rs.at[mine], ss.at[event], sr.at[event], dev(yy, xx))
+    sends = []
+
+    def ship(src, dst, event, to):
+        copy = send(src, dst, ss.at[event], sr.at[event], dev(*to))
         copy.start()
         sends.append(copy)
 
-    pair(y)
-    give(y, xo, 0)
+    def give(yy, xx, rows, event):
+        ship(part.at[slot(yy, xx), rows], rs.at[mine, rows], event, (yy, xx))
+
+    def taken(dst, event):
+        landed(dst, ss.at[event], sr.at[event], dev(y, xo))
+
+    widen(0, y)
     arrive(slot(ym, xo), None, 3)
     forward(slot(ym, xo), half[0], 7, (yp, x))
     arrive(slot(yp, xo), None, 4)
     forward(slot(yp, xo), half[1], 8, (ym, x))
-    pair(ym)
-    give(ym, x, 1)
-    give(ym, xo, 2)
-    pair(yp)
-    give(yp, x, 3)
-    give(yp, xo, 4)
+    relay.stage4()
+    widen(1, ym)
+    widen(2, yp)
+    relay.stage5()
+    narrow(0, y)
+    give(y, xo, pl.ds(0, TD), 0)
+    narrow(1, ym)
+    for k, xx in enumerate((x, xo)):
+        give(ym, xx, half[0], 1 + k)
+    narrow(2, yp)
+    for k, xx in enumerate((x, xo)):
+        give(yp, xx, half[1], 3 + k)
     arrive(slot(y2, x), half[0], 5)
     arrive(slot(y2, x), half[1], 6)
     arrive(slot(y2, xo), half[0], 7)
     arrive(slot(y2, xo), half[1], 8)
-    pair(y2)
-    give(y2, x, 5)
-    give(y2, xo, 6)
-    for event, src in enumerate([(y, xo), (yp, x), (yp, xo), (ym, x), (ym, xo), (y2, x), (y2, xo)]):
-        landed(rs.at[slot(*src)], ss.at[event], sr.at[event], dev(*src))
-    rs[mine] = part[mine]
+    widen(3, y2)
+    narrow(3, y2)
+    for k, xx in enumerate((xo, x)):
+        ship(part.at[slot(y2, xx), half[0]], via.at[0, k], 5 + k, (yp, x))
+        ship(part.at[slot(y2, xx), half[1]], via.at[1, k], 7 + k, (ym, x))
+    for k, xx in enumerate((xo, x)):
+        for side, (yy, event) in enumerate(((yp, 9), (ym, 11))):
+            taken(via.at[side, k], 5 + 2 * side + k)
+            ref = part.at[slot(yy, xx), half[side]]
+            ref[...] = (ref[...].astype(F32) + via[side, k].astype(F32)).astype(BF)
+            give(yy, xx, half[side], event + k)
+    taken(rs.at[slot(y, xo)], 0)
+    for k, xx in enumerate((x, xo)):
+        taken(rs.at[slot(yp, xx), half[0]], 1 + k)
+        taken(rs.at[slot(ym, xx), half[1]], 3 + k)
+    for k, xx in enumerate((xo, x)):
+        taken(rs.at[slot(ym, xx), half[0]], 9 + k)
+        taken(rs.at[slot(yp, xx), half[1]], 11 + k)
+    sources = [slot(y, xo), slot(ym, x), slot(ym, xo), slot(yp, x), slot(yp, xo)]
 
     def close(n, carry):
         cols = pl.ds(pl.multiple_of(n * 256, 256), 256)
-        total = rs[0, :, cols].astype(F32)
-        for c in range(1, 8):
+        total = part[mine, :, cols].astype(F32)
+        for c in sources:
             total = total + rs[c, :, cols].astype(F32)
         out[:, cols] = (hid[:, cols] + total).astype(BF)
         return carry
@@ -595,6 +616,7 @@
     lax.fori_loop(0, 8, close, 0)
     for copy in started + sends:
         copy.wait_send()
+    relay.finish()
 
 
 def run_mlp(att, tok, gain, wo, wg, wu, wd):
@@ -609,13 +631,14 @@
             pltpu.VMEM((D, D), BF),
             pltpu.VMEM((D, HB), BF),
             pltpu.VMEM((D, HB), BF),
-            pltpu.VMEM((HB, D), BF),
+            pltpu.VMEM((8, 2, 64, D), BF),
             pltpu.VMEM((TD, D), F32),
             pltpu.VMEM((8, TD, D), BF),
-            pltpu.VMEM((256, HB), BF),
+            pltpu.VMEM((4, 256, HB), BF),
             pltpu.VMEM((8, TD, D), BF),
             pltpu.VMEM((8, TD, D), BF),
-            dma((4,)), dma((9,)), dma((9,)), dma((7,)), dma((7,)),
+            pltpu.VMEM((2, 2, 64, D), BF),
+            dma((4,)), dma((9,)), dma((9,)), dma((13,)), dma((13,)), dma((30,)), dma((16, 2)),
         ],
         compiler_params=pltpu.CompilerParams(
             collective_id=3, has_side_effects=True, vmem_limit_bytes=VLIM
@@ -632,10 +655,10 @@
         tokens, attn_gain.reshape(1, D), query_weight, keyval_weight,
         gate_rows, up_rows, down_rows, valid.reshape(1, TD),
     )
-    att, cache, wg, wu, wd = run_attend(qkv, flags, kvrows, lengths, page_table, wg, wu, wd)
+    att, cache, wg, wu = run_attend(qkv, flags, kvrows, lengths, page_table, wg, wu)
     layer_out = run_mlp(
         att, tokens, mlp_gain.reshape(1, D), output_weight,
-        wg.reshape(D, HB), wu.reshape(D, HB), wd.reshape(HB, D),
+        wg.reshape(D, HB), wu.reshape(D, HB), wd,
     )
     return (layer_out, cache[None, None])
 

time: 198 us -> 177 us (0.89)
  Pallas kernels: 193 us -> 171 us
    pallas_call x1, Pallas kernels: 74.2 us -> 55.1 us  [run_attend(): pl.pallas_call(attend, out_shape=(sds((NMP, TD, 128), BF), sds((NDP, 2, 1...]
    pallas_call x1, Pallas kernels: 92 us -> 88.9 us  [run_mlp(): pl.pallas_call(mlp, out_shape=jax.ShapeDtypeStruct((TD, D), BF), in_specs...]
where the time goes in v2:
time: 177 us; the launch traced here: 176 us
  Pallas kernels  171 us (97%)
  local copies, waits for them, and re-layouts  4 us (2%)
    pallas_call x1, Pallas kernels, run_mlp(): pl.pallas_call(mlp, out_shape=jax.ShapeDtypeStruct((TD, D), BF), in_specs...  88.9 us
    pallas_call x1, Pallas kernels, run_attend(): pl.pallas_call(attend, out_shape=(sds((NMP, TD, 128), BF), sds((NDP, 2, 1...  55.1 us
    pallas_call x1, Pallas kernels, run_front(): pl.pallas_call(front, out_shape=(sds((NMP, 2, TD, 128), BF), sds((NMP, 16...  26.6 us
    unnamed x5, local copies, waits for them, and re-layouts  4 us

profile of v2, /device:TPU:0, one launch (start us, length us, event | category | flops | bytes accessed | tf_op | source)
XLA Modules:
  0.0 176.0 jit_solution(816584569288089571)
XLA Ops:
  1.3 1.3 copy.16.table
  2.6 26.6 %front.1 = (bf16[16,2,128,128]{3,2,1,0:T(8,128)(2,1)}, bf16[16,16,128]{2,1,0:T(8,128)(2,1)}, bf16[8,8,2,16,1024]{4,3,2,1,0:T(8,128)(2,1)}, bf16[8,8,2,16,1024]{4...) custom-call(bf16[128,2048]{1,0:T(8,128)(2,1)} %tok.3, f32[1,2048]{1,0:T(1,128)} %bitcast.9, ...), custom_call_target="tpu_custom_call" | custom-call | tf_op jit(solution)/shard_map/front/pallas_call | solution.py:166
  29.2 55.1 %attend.1 = (bf16[16,128,128]{2,1,0:T(8,128)(2,1)}, bf16[8,2,16,1024]{3,2,1,0:T(8,128)(2,1)}, bf16[8,8,2,16,1024]{4,3,2,1,0:T(8,128)(2,1)}, bf16[8,8,2,16,1024]{4,3,2,1,0:T(8,128)(2,1)}) custom-call(bf16[16,2,128,128]{3,2,1,0:T(8,128)(2,1)} %get-tuple-element.12.qkv, ...), custom_call_target="tpu_custom_call", output_to_operand_aliasing={{2}: (5, {}), {3}: (6, {})} | custom-call | tf_op jit(solution)/shard_map/attend/pallas_call | solution.py:427
  84.4 0.0 copy-start
  84.4 88.9 %mlp.1 = bf16[128,2048]{1,0:T(8,128)(2,1)} custom-call(bf16[16,128,128]{2,1,0:T(8,128)(2,1)} %get-tuple-element.17.att, bf16[128,2048]{1,0:T(8,128)(2,1)} %tok.3, f32[1,2048]{1,0:T(1,128)} %bitcast.10, bf16[2048,2048]{1,0:T(8,128)(2,1)} %wo.1, bf16[2048,1024]{1,0:T(8,128)(2,1)} %bitcast.6, bf16[2048,1024]{1,0:T(8,128)(2,1)} %bitcast.7, ...), custom_call_target="tpu_custom_call" | custom-call | tf_op jit(solution)/shard_map/mlp/pallas_call | solution.py:624
  173.3 1.9 %copy.22 = bf16[128,2048]{1,0:T(8,128)(2,1)} copy(bf16[128,2048]{1,0:T(8,128)(2,1)} %mlp.1) | data formatting | bytes 1048576
  175.2 0.0 copy-done
  175.2 0.8 copy.23
Async XLA Ops:
  84.4 90.8 %copy-start = (bf16[8,2,16,1024]{3,2,1,0:T(8,128)(2,1)S(1)}, bf16[8,2,16,1024]{3,2,1,0:T(8,128)(2,1)}, u32[]{:S(2)}) copy-start(bf16[8,2,16,1024]{3,2,1,0:T(8,128)(2,1)} %get-tuple-element.21) | copy-start | bytes 1572868

commit v3 on v2

--- a/solution.py
+++ b/solution.py
@@ -17,6 +17,7 @@
 D = 2048
 HB = 1024
 NEG = -1e30
+INNER = 16
 ANY = pl.BlockSpec(memory_space=pl.ANY)
 VM = pl.BlockSpec(memory_space=pltpu.VMEM)
 SM = pl.BlockSpec(memory_space=pltpu.SMEM)
@@ -470,32 +471,35 @@
     relay = Relay(lambda b, c, p: wd_v.at[b, c, pl.ds(p * 32, 32)], wss, wsr)
     barrier, count = greet([dev(*p) for p in peers] + [relay.partner, relay.up, relay.down, relay.across])
     loads = [
-        pltpu.make_async_copy(wo, wo_v, wsem.at[0]),
-        pltpu.make_async_copy(wg, wg_v, wsem.at[1]),
-        pltpu.make_async_copy(wu, wu_v, wsem.at[2]),
-        pltpu.make_async_copy(wd, wd_v.at[dp, core], wsem.at[3]),
+        pltpu.make_async_copy(wg, wg_v, wsem.at[0]),
+        pltpu.make_async_copy(wu, wu_v, wsem.at[1]),
+        pltpu.make_async_copy(wd, wd_v.at[dp, core], wsem.at[2]),
     ]
-    loads[3].start()
-    for copy in loads[:3]:
+    wo_loads = [
+        pltpu.make_async_copy(wo.at[:, pl.ds(n * 512, 512)], wo_v.at[n], wsem.at[3 + n]) for n in range(4)
+    ]
+    loads[2].start()
+    for copy in wo_loads:
         copy.start()
     pl.semaphore_wait(barrier, count)
-    loads[3].wait()
+    loads[2].wait()
     relay.stage0()
     for j in range(NMP):
         att_v[:, j * 128 : (j + 1) * 128] = att[j]
-    loads[0].wait()
-
-    def project(n, carry):
-        cols = pl.ds(pl.multiple_of(n * 512, 512), 512)
-        got = jnp.dot(att_v[...], wo_v[:, cols], preferred_element_type=F32)
+    for n in range(4):
+        cols = slice(n * 512, (n + 1) * 512)
+        wo_loads[n].wait()
+        got = jnp.dot(att_v[...], wo_v[n], preferred_element_type=F32)
         hid[:, cols] = (tok[:, cols].astype(F32) + got).astype(BF).astype(F32)
-        return carry
-
-    lax.fori_loop(0, 4, project, 0)
+    for copy in loads[:2]:
+        copy.start()
     act[chip] = norm_rows(hid[...], gain[...]).astype(BF)
 
     started = []
     half = (pl.ds(0, 64), pl.ds(64, 64))
+    inner = (pl.ds(64 - INNER, INNER), pl.ds(64, INNER))
+    both = pl.ds(64 - INNER, 2 * INNER)
+    outer = (pl.ds(0, 64 - INNER), pl.ds(64 + INNER, 64 - INNER))
 
     def forward(block, rows, event, to):
         ref = act.at[block] if rows is None else act.at[block, rows]
@@ -517,14 +521,17 @@
     relay.stage2()
     relay.stage1()
     arrive(slot(y, xo), None, 0)
-    forward(slot(y, xo), None, 3, (yp, x))
-    forward(slot(y, xo), None, 4, (ym, x))
+    for i in range(2):
+        forward(slot(y, xo), outer[i], 3 + i, (yp, x))
+        forward(slot(y, xo), outer[i], 5 + i, (ym, x))
     arrive(slot(ym, x), None, 1)
-    forward(slot(ym, x), half[0], 5, (yp, x))
+    forward(slot(ym, x), half[0], 7, (yp, x))
+    forward(slot(ym, x), both, 9, (y, xo))
     arrive(slot(yp, x), None, 2)
-    forward(slot(yp, x), half[1], 6, (ym, x))
+    forward(slot(yp, x), half[1], 8, (ym, x))
+    forward(slot(yp, x), both, 10, (y, xo))
     relay.stage3()
-    for copy in loads[1:3]:
+    for copy in loads[:2]:
         copy.wait()
 
     def widen(k, yy):
@@ -565,12 +572,20 @@
         landed(dst, ss.at[event], sr.at[event], dev(y, xo))
 
     widen(0, y)
-    arrive(slot(ym, xo), None, 3)
-    forward(slot(ym, xo), half[0], 7, (yp, x))
-    arrive(slot(yp, xo), None, 4)
-    forward(slot(yp, xo), half[1], 8, (ym, x))
+    arrive(slot(ym, xo), outer[0], 3)
+    forward(slot(ym, xo), outer[0], 11, (yp, x))
+    arrive(slot(yp, xo), outer[1], 6)
+    forward(slot(yp, xo), outer[1], 12, (ym, x))
     relay.stage4()
+    arrive(slot(ym, xo), outer[1], 4)
+    arrive(slot(ym, xo), both, 9)
     widen(1, ym)
+    arrive(slot(y2, x), half[0], 7)
+    forward(slot(y2, x), inner[0], 13, (y, xo))
+    arrive(slot(y2, x), half[1], 8)
+    forward(slot(y2, x), inner[1], 14, (y, xo))
+    arrive(slot(yp, xo), outer[0], 5)
+    arrive(slot(yp, xo), both, 10)
     widen(2, yp)
     relay.stage5()
     narrow(0, y)
@@ -581,10 +596,9 @@
     narrow(2, yp)
     for k, xx in enumerate((x, xo)):
         give(yp, xx, half[1], 3 + k)
-    arrive(slot(y2, x), half[0], 5)
-    arrive(slot(y2, x), half[1], 6)
-    arrive(slot(y2, xo), half[0], 7)
-    arrive(slot(y2, xo), half[1], 8)
+    for i in range(2):
+        arrive(slot(y2, xo), outer[i], 11 + i)
+        arrive(slot(y2, xo), inner[i], 13 + i)
     widen(3, y2)
     narrow(3, y2)
     for k, xx in enumerate((xo, x)):
@@ -628,7 +642,7 @@
         out_specs=VM,
         scratch_shapes=[
             pltpu.VMEM((TD, D), BF),
-            pltpu.VMEM((D, D), BF),
+            pltpu.VMEM((4, D, 512), BF),
             pltpu.VMEM((D, HB), BF),
             pltpu.VMEM((D, HB), BF),
             pltpu.VMEM((8, 2, 64, D), BF),
@@ -638,7 +652,7 @@
             pltpu.VMEM((8, TD, D), BF),
             pltpu.VMEM((8, TD, D), BF),
             pltpu.VMEM((2, 2, 64, D), BF),
-            dma((4,)), dma((9,)), dma((9,)), dma((13,)), dma((13,)), dma((30,)), dma((16, 2)),
+            dma((7,)), dma((15,)), dma((15,)), dma((13,)), dma((13,)), dma((30,)), dma((16, 2)),
         ],
         compiler_params=pltpu.CompilerParams(
             collective_id=3, has_side_effects=True, vmem_limit_bytes=VLIM

time: 177 us -> 177 us (level)
  no operation moved by 1% of the time
where the time goes in v3:
time: 177 us; the launch traced here: 176 us
  Pallas kernels  171 us (97%)
  local copies, waits for them, and re-layouts  4 us (2%)
    pallas_call x1, Pallas kernels, run_mlp(): pl.pallas_call(mlp, out_shape=jax.ShapeDtypeStruct((TD, D), BF), in_specs...  88.8 us
    pallas_call x1, Pallas kernels, run_attend(): pl.pallas_call(attend, out_shape=(sds((NMP, TD, 128), BF), sds((NDP, 2, 1...  55.1 us
    pallas_call x1, Pallas kernels, run_front(): pl.pallas_call(front, out_shape=(sds((NMP, 2, TD, 128), BF), sds((NMP, 16...  26.6 us
    unnamed x5, local copies, waits for them, and re-layouts  4 us

profile of v3, /device:TPU:0, one launch (start us, length us, event | category | flops | bytes accessed | tf_op | source)
XLA Modules:
  0.0 175.9 jit_solution(12288030902440128367)
XLA Ops:
  1.3 1.3 copy.16.table
  2.6 26.6 %front.1 = (bf16[16,2,128,128]{3,2,1,0:T(8,128)(2,1)}, bf16[16,16,128]{2,1,0:T(8,128)(2,1)}, bf16[8,8,2,16,1024]{4,3,2,1,0:T(8,128)(2,1)}, bf16[8,8,2,16,1024]{4...) custom-call(bf16[128,2048]{1,0:T(8,128)(2,1)} %tok.3, f32[1,2048]{1,0:T(1,128)} %bitcast.9, ...), custom_call_target="tpu_custom_call" | custom-call | tf_op jit(solution)/shard_map/front/pallas_call | solution.py:167
  29.2 55.1 %attend.1 = (bf16[16,128,128]{2,1,0:T(8,128)(2,1)}, bf16[8,2,16,1024]{3,2,1,0:T(8,128)(2,1)}, bf16[8,8,2,16,1024]{4,3,2,1,0:T(8,128)(2,1)}, bf16[8,8,2,16,1024]{4,3,2,1,0:T(8,128)(2,1)}) custom-call(bf16[16,2,128,128]{3,2,1,0:T(8,128)(2,1)} %get-tuple-element.12.qkv, ...), custom_call_target="tpu_custom_call", output_to_operand_aliasing={{2}: (5, {}), {3}: (6, {})} | custom-call | tf_op jit(solution)/shard_map/attend/pallas_call | solution.py:428
  84.4 0.0 copy-start
  84.4 88.8 %mlp.1 = bf16[128,2048]{1,0:T(8,128)(2,1)} custom-call(bf16[16,128,128]{2,1,0:T(8,128)(2,1)} %get-tuple-element.17.att, bf16[128,2048]{1,0:T(8,128)(2,1)} %tok.3, f32[1,2048]{1,0:T(1,128)} %bitcast.10, bf16[2048,2048]{1,0:T(8,128)(2,1)} %wo.1, bf16[2048,1024]{1,0:T(8,128)(2,1)} %bitcast.6, bf16[2048,1024]{1,0:T(8,128)(2,1)} %bitcast.7, ...), custom_call_target="tpu_custom_call" | custom-call | tf_op jit(solution)/shard_map/mlp/pallas_call | solution.py:638
  173.2 1.9 %copy.22 = bf16[128,2048]{1,0:T(8,128)(2,1)} copy(bf16[128,2048]{1,0:T(8,128)(2,1)} %mlp.1) | data formatting | bytes 1048576
  175.1 0.0 copy-done
  175.1 0.8 copy.23
Async XLA Ops:
  84.4 90.7 %copy-start = (bf16[8,2,16,1024]{3,2,1,0:T(8,128)(2,1)S(1)}, bf16[8,2,16,1024]{3,2,1,0:T(8,128)(2,1)}, u32[]{:S(2)}) copy-start(bf16[8,2,16,1024]{3,2,1,0:T(8,128)(2,1)} %get-tuple-element.21) | copy-start | bytes 1572868

commit v4 on v3

--- a/solution.py
+++ b/solution.py
@@ -547,7 +547,7 @@
 
         lax.fori_loop(0, 4, hidden, 0)
 
-    def narrow(k, yy):
+    def narrow(k, yy, start=0, stop=4):
         def final(n, carry):
             cols = pl.ds(pl.multiple_of(n * 512, 512), 512)
             w = wd_v[:, :, :, cols].reshape(HB, 512)
@@ -556,7 +556,7 @@
             part[yy * 2 + 1, :, cols] = r[TD:]
             return carry
 
-        lax.fori_loop(0, 4, final, 0)
+        lax.fori_loop(start, stop, final, 0)
 
     sends = []
 
@@ -588,8 +588,6 @@
     arrive(slot(yp, xo), both, 10)
     widen(2, yp)
     relay.stage5()
-    narrow(0, y)
-    give(y, xo, pl.ds(0, TD), 0)
     narrow(1, ym)
     for k, xx in enumerate((x, xo)):
         give(ym, xx, half[0], 1 + k)
@@ -600,23 +598,30 @@
         arrive(slot(y2, xo), outer[i], 11 + i)
         arrive(slot(y2, xo), inner[i], 13 + i)
     widen(3, y2)
-    narrow(3, y2)
-    for k, xx in enumerate((xo, x)):
-        ship(part.at[slot(y2, xx), half[0]], via.at[0, k], 5 + k, (yp, x))
-        ship(part.at[slot(y2, xx), half[1]], via.at[1, k], 7 + k, (ym, x))
-    for k, xx in enumerate((xo, x)):
-        for side, (yy, event) in enumerate(((yp, 9), (ym, 11))):
-            taken(via.at[side, k], 5 + 2 * side + k)
-            ref = part.at[slot(yy, xx), half[side]]
-            ref[...] = (ref[...].astype(F32) + via[side, k].astype(F32)).astype(BF)
-            give(yy, xx, half[side], event + k)
+    wide = (pl.ds(0, 1024), pl.ds(1024, 1024))
+    for c in range(2):
+        narrow(3, y2, 2 * c, 2 * c + 2)
+        for k, xx in enumerate((xo, x)):
+            ship(part.at[slot(y2, xx), half[0], wide[c]], via.at[0, k, :, wide[c]], 5 + 8 * c + k, (yp, x))
+            ship(part.at[slot(y2, xx), half[1], wide[c]], via.at[1, k, :, wide[c]], 7 + 8 * c + k, (ym, x))
+    narrow(0, y)
+    give(y, xo, pl.ds(0, TD), 0)
+    for c in range(2):
+        for k, xx in enumerate((xo, x)):
+            for side, (yy, event) in enumerate(((yp, 9), (ym, 11))):
+                got = via.at[side, k, :, wide[c]]
+                taken(got, 5 + 8 * c + 2 * side + k)
+                ref = part.at[slot(yy, xx), half[side], wide[c]]
+                ref[...] = (ref[...].astype(F32) + got[...].astype(F32)).astype(BF)
+                ship(ref, rs.at[mine, half[side], wide[c]], event + 8 * c + k, (yy, xx))
     taken(rs.at[slot(y, xo)], 0)
     for k, xx in enumerate((x, xo)):
         taken(rs.at[slot(yp, xx), half[0]], 1 + k)
         taken(rs.at[slot(ym, xx), half[1]], 3 + k)
-    for k, xx in enumerate((xo, x)):
-        taken(rs.at[slot(ym, xx), half[0]], 9 + k)
-        taken(rs.at[slot(yp, xx), half[1]], 11 + k)
+    for c in range(2):
+        for k, xx in enumerate((xo, x)):
+            taken(rs.at[slot(ym, xx), half[0], wide[c]], 9 + 8 * c + k)
+            taken(rs.at[slot(yp, xx), half[1], wide[c]], 11 + 8 * c + k)
     sources = [slot(y, xo), slot(ym, x), slot(ym, xo), slot(yp, x), slot(yp, xo)]
 
     def close(n, carry):
@@ -652,7 +657,7 @@
             pltpu.VMEM((8, TD, D), BF),
             pltpu.VMEM((8, TD, D), BF),
             pltpu.VMEM((2, 2, 64, D), BF),
-            dma((7,)), dma((15,)), dma((15,)), dma((13,)), dma((13,)), dma((30,)), dma((16, 2)),
+            dma((7,)), dma((15,)), dma((15,)), dma((21,)), dma((21,)), dma((30,)), dma((16, 2)),
         ],
         compiler_params=pltpu.CompilerParams(
             collective_id=3, has_side_effects=True, vmem_limit_bytes=VLIM

time: 177 us -> 174 us (0.983)
  Pallas kernels: 171 us -> 168 us
    pallas_call x1, Pallas kernels: 88.8 us -> 86.4 us  [run_mlp(): pl.pallas_call(mlp, out_shape=jax.ShapeDtypeStruct((TD, D), BF), in_specs...]
where the time goes in v4:
time: 174 us; the launch traced here: 173 us
  Pallas kernels  168 us (97%)
  local copies, waits for them, and re-layouts  4 us (2%)
    pallas_call x1, Pallas kernels, run_mlp(): pl.pallas_call(mlp, out_shape=jax.ShapeDtypeStruct((TD, D), BF), in_specs...  86.4 us
    pallas_call x1, Pallas kernels, run_attend(): pl.pallas_call(attend, out_shape=(sds((NMP, TD, 128), BF), sds((NDP, 2, 1...  55.1 us
    pallas_call x1, Pallas kernels, run_front(): pl.pallas_call(front, out_shape=(sds((NMP, 2, TD, 128), BF), sds((NMP, 16...  26.6 us
    unnamed x5, local copies, waits for them, and re-layouts  4 us

profile of v4, /device:TPU:0, one launch (start us, length us, event | category | flops | bytes accessed | tf_op | source)
XLA Modules:
  0.0 173.5 jit_solution(18307551433504289037)
XLA Ops:
  1.3 1.3 copy.16.table
  2.6 26.6 %front.1 = (bf16[16,2,128,128]{3,2,1,0:T(8,128)(2,1)}, bf16[16,16,128]{2,1,0:T(8,128)(2,1)}, bf16[8,8,2,16,1024]{4,3,2,1,0:T(8,128)(2,1)}, bf16[8,8,2,16,1024]{4...) custom-call(bf16[128,2048]{1,0:T(8,128)(2,1)} %tok.3, f32[1,2048]{1,0:T(1,128)} %bitcast.9, ...), custom_call_target="tpu_custom_call" | custom-call | tf_op jit(solution)/shard_map/front/pallas_call | solution.py:167
  29.2 55.1 %attend.1 = (bf16[16,128,128]{2,1,0:T(8,128)(2,1)}, bf16[8,2,16,1024]{3,2,1,0:T(8,128)(2,1)}, bf16[8,8,2,16,1024]{4,3,2,1,0:T(8,128)(2,1)}, bf16[8,8,2,16,1024]{4,3,2,1,0:T(8,128)(2,1)}) custom-call(bf16[16,2,128,128]{3,2,1,0:T(8,128)(2,1)} %get-tuple-element.12.qkv, ...), custom_call_target="tpu_custom_call", output_to_operand_aliasing={{2}: (5, {}), {3}: (6, {})} | custom-call | tf_op jit(solution)/shard_map/attend/pallas_call | solution.py:428
  84.4 0.0 copy-start
  84.4 86.4 %mlp.1 = bf16[128,2048]{1,0:T(8,128)(2,1)} custom-call(bf16[16,128,128]{2,1,0:T(8,128)(2,1)} %get-tuple-element.17.att, bf16[128,2048]{1,0:T(8,128)(2,1)} %tok.3, f32[1,2048]{1,0:T(1,128)} %bitcast.10, bf16[2048,2048]{1,0:T(8,128)(2,1)} %wo.1, bf16[2048,1024]{1,0:T(8,128)(2,1)} %bitcast.6, bf16[2048,1024]{1,0:T(8,128)(2,1)} %bitcast.7, ...), custom_call_target="tpu_custom_call" | custom-call | tf_op jit(solution)/shard_map/mlp/pallas_call | solution.py:643
  170.8 1.9 %copy.22 = bf16[128,2048]{1,0:T(8,128)(2,1)} copy(bf16[128,2048]{1,0:T(8,128)(2,1)} %mlp.1) | data formatting | bytes 1048576
  172.7 0.0 copy-done
  172.7 0.8 copy.23
Async XLA Ops:
  84.4 88.3 %copy-start = (bf16[8,2,16,1024]{3,2,1,0:T(8,128)(2,1)S(1)}, bf16[8,2,16,1024]{3,2,1,0:T(8,128)(2,1)}, u32[]{:S(2)}) copy-start(bf16[8,2,16,1024]{3,2,1,0:T(8,128)(2,1)} %get-tuple-element.21) | copy-start | bytes 1572868
